TPU v7x, 512 devices: a whole 4x4x16 slice. The times are simulated.
512 devices in a mesh: site: 32 (over x_lo, z), sector: 16 (over y, x_hi, core).
Axes of the slice: x: 4 (x_hi: 2, x_lo: 2; x = x_hi * 2 + x_lo), y: 4, z: 16, core: 2. Of those that a mesh axis runs over, the one named last changes fastest.
Arguments:
- site_tensors: bfloat16 [32, 2, 6144, 384], P('site', None, 'sector'), may hold values from -0.21875 to 0.21875
- environments: bfloat16 [32, 5, 6144, 384], P('site', None, 'sector'), may hold values from -6 to 6
- mpo: float32 [32, 5, 5, 2, 2], P('site'), may hold values from -4 to 4
- boundary: bfloat16 [5, 6144, 384], P(None, 'sector'), may hold values from -6 to 6
Outputs:
- environments_out: bfloat16 [32, 5, 6144, 384], P('site', None, 'sector')
All inputs are finite; a program needn't handle non-finite values.
Results may differ from a plain program's by a relative error of at most 0.0054.
Values may be sent and summed in bfloat16 or wider, within the bound.
No kernel may reach another device: no remote copies, remote signals or barrier semaphores. Data moves between devices by JAX's collectives and lax.ppermute only.
A program may use at most 64 MiB of HBM per device.

v0:
```python
import jax
import jax.numpy as jnp
import numpy as np
from jax import lax
from jax.sharding import PartitionSpec as P

W = 5


charge_steps = (0, 1, -1, 0, 0)


def shifted(value, axis, steps):
    count = lax.axis_size(axis)
    first, last = (max(0, -steps), min(count, count - steps))
    return lax.ppermute(value, axis, [(source, source + steps) for source in range(first, last)])


def extended(cells, sides, width):
    for axis, dim in sides:
        count = lax.axis_size(axis)
        head = lax.slice_in_dim(cells, 0, width, axis=dim)
        tail = lax.slice_in_dim(cells, cells.shape[dim] - width, cells.shape[dim], axis=dim)
        cells = jnp.concatenate(
            [
                lax.ppermute(tail, axis, [(i, (i + 1) % count) for i in range(count)]),
                cells,
                lax.ppermute(head, axis, [((i + 1) % count, i) for i in range(count)]),
            ],
            axis=dim,
        )
    return cells


def from_behind(value, axis, steps):
    count = lax.axis_size(axis)
    pairs = [(source, (source + steps) % count) for source in range(count)]
    return lax.ppermute(value, axis, pairs)


def allowed():
    charges = np.array(charge_steps)
    spins = np.arange(2)
    differ = charges[None, :] - charges[:, None]
    return (
        spins[None, None, None, :] - spins[None, None, :, None] == differ[:, :, None, None]
    ).astype(np.float32)


def pick_blocks(near_blocks, sector_width):
    return jnp.stack(
        [
            near_blocks[
                :, (1 + charge_steps[term]) * sector_width : (2 + charge_steps[term]) * sector_width
            ]
            for term in range(W)
        ]
    )


def receive_env(state, boundary, at_start):
    arrived = shifted(state, "site", 1)
    return jnp.where(at_start, boundary, arrived)


def local(site_tensors, environments, mpo, boundary):
    blocks = site_tensors[0]
    sector_width = blocks.shape[2]
    couplings = mpo[0] * allowed()
    near_blocks = extended(blocks, (("sector", 1),), sector_width)
    own_stack = pick_blocks(near_blocks, sector_width)
    at_start = lax.axis_index("site") == 0
    state = environments[0]
    incoming = receive_env(state, boundary, at_start)
    products = jnp.einsum("wab,wtbc->wtac", incoming, own_stack, preferred_element_type=jnp.float32)
    combined = jnp.einsum(
        "wvst,wtac->vsac", couplings, products, precision=lax.Precision.HIGHEST
    ).astype(jnp.bfloat16)
    own_part = jnp.einsum(
        "ba,vbc->vac", blocks[0], combined[:, 0], preferred_element_type=jnp.float32
    )
    carried_part = jnp.einsum(
        "ba,vbc->vac", blocks[1], combined[:, 1], preferred_element_type=jnp.float32
    ).astype(jnp.bfloat16)
    carried = jnp.stack([from_behind(carried_part[term], "sector", 1) for term in range(W)])
    state = (own_part + carried.astype(jnp.float32)).astype(jnp.bfloat16)
    return state[None]


def solution(mesh):
    in_specs = (
        P("site", None, "sector", None),
        P("site", None, "sector", None),
        P("site", None, None, None, None),
        P(None, "sector", None),
    )
    out_specs = P("site", None, "sector", None)
    return jax.shard_map(local, mesh=mesh, in_specs=in_specs, out_specs=out_specs, check_vma=False)
```

profile of v0, /device:TPU:24, one launch (start us, length us, event | category | flops | bytes accessed | tf_op | source)
XLA Modules:
  0.0 115.9 jit_solution(4588908812894996552)
XLA Ops:
  0.0 0.0 copy-start
  0.0 4.0 %collective-permute-start.2 = (bf16[5,384,384]{2,1,0:T(8,128)(2,1)}, bf16[5,384,384]{2,1,0:T(8,128)(2,1)S(1)}, u32[]{:S(2)}, u32[]{:S(2)}) collective-permute-start(bf16[5,384,384]{2,1,0:T(8,128)(2,1)} %bitcast.72), channel_id=1, source_target_pairs={{0,16},{16,32},{32,48},{48,64},{64,80},{80,96},{96,112},{112,128},... | collective-permute-start | bytes 4423688 | tf_op jit(solution)/shard_map/ppermute | solution.py:16
  4.0 4.3 %collective-permute-start = (bf16[2,384,384]{2,1,0:T(8,128)(2,1)}, bf16[2,384,384]{2,1,0:T(8,128)(2,1)S(1)}, u32[]{:S(2)}, u32[]{:S(2)}) collective-permute-start(bf16[2,384,384]{2,1,0:T(8,128)(2,1)} %bitcast.70), channel_id=1, source_target_pairs={{1,0},{2,1},{3,2},{4,3},{5,4},{6,5},{7,6},{8,7},{9,8},{10,9},{11,1... | collective-permute-start | bytes 1769480 | tf_op jit(solution)/shard_map/ppermute | solution.py:28
  8.3 1.9 %collective-permute-start.1 = (bf16[2,384,384]{2,1,0:T(8,128)(2,1)}, bf16[2,384,384]{2,1,0:T(8,128)(2,1)S(1)}, u32[]{:S(2)}, u32[]{:S(2)}) collective-permute-start(bf16[2,384,384]{2,1,0:T(8,128)(2,1)} %bitcast.71), channel_id=1, source_target_pairs={{0,1},{1,2},{2,3},{3,4},{4,5},{5,6},{6,7},{7,8},{8,9},{9,10},{10,1... | collective-permute-start | bytes 1769480 | tf_op jit(solution)/shard_map/ppermute | solution.py:26
  10.3 1.1 constant_dynamic-update-slice_fusion.2
  11.4 0.7 multiply_bitcast_fusion
  12.1 0.0 copy-start.1
  12.1 39.9 %collective-permute-done = bf16[2,384,384]{2,1,0:T(8,128)(2,1)S(1)} collective-permute-done((bf16[2,384,384]{2,1,0:T(8,128)(2,1)}, bf16[2,384,384]{2,1,0:T(8,128)(2,1)S(1)}, u32[]{:S(2)}, u32[]{:S(2)}) %collective-permute-start) | collective-permute-done | bytes 589856 | tf_op jit(solution)/shard_map/ppermute | solution.py:28
  52.0 0.1 bitcast_dynamic-update-slice_fusion.1
  52.1 3.0 %collective-permute-done.1 = bf16[2,384,384]{2,1,0:T(8,128)(2,1)S(1)} collective-permute-done((bf16[2,384,384]{2,1,0:T(8,128)(2,1)}, bf16[2,384,384]{2,1,0:T(8,128)(2,1)S(1)}, u32[]{:S(2)}, u32[]{:S(2)}) %collective-permute-start.1) | collective-permute-done | bytes 589856 | tf_op jit(solution)/shard_map/ppermute | solution.py:26
  55.1 0.1 bitcast_dynamic-update-slice_fusion
  55.2 0.0 copy-done
  55.3 0.1 constant_dynamic-update-slice_fusion.1
  55.4 0.1 constant_dynamic-update-slice_fusion
  55.5 0.0 collective-permute-done.2
  55.5 0.0 copy-done.1
  55.5 4.9 %fusion.5 = f32[5,2,384,384]{3,2,1,0:T(8,128)} fusion(bf16[5,2,384,384]{3,2,1,0:T(8,128)(2,1)S(1)} %constant_dynamic-update-slice_fusion, bf16[5,384,384]{2,1,0:T(8,128)(2,1)S(1)} %copy-done.1, bf16[5,384,384]{2,1,0:T(8,128)(2,1)S(1)} %collective-permute-done.2, pred[]{:T(512)S(6)} %eq.3), kind=kOutput, calls=%fused_computation.8 | convolution fusion | flops 1133199360 | bytes 11796481 | tf_op jit(solution)/shard_map/wab,wtbc->wtac/dot_general | solution.py:75
  60.4 8.7 %copy.11 = f32[5,2,384,384]{2,0,1,3:T(8,128)} copy(f32[5,2,384,384]{3,2,1,0:T(8,128)} %fusion.5) | data formatting | bytes 11796480 | tf_op jit(solution)/shard_map/wab,wtbc->wtac/dot_general | solution.py:75
  69.1 17.9 %bitcast_convert_fusion = bf16[5,2,384,384]{3,0,2,1:T(8,128)(2,1)S(1)} fusion(f32[5,2,384,384]{2,0,1,3:T(8,128)} %copy.11, f32[5,5,2,2,1]{1,3,2,0,4:T(2,128)S(1)} %multiply_bitcast_fusion), kind=kOutput, calls=%fused_computation.2 | convolution fusion | flops 178421760 | bytes 8847760 | tf_op jit(solution)/shard_map/wvst,wtac->vsac/dot_general | solution.py:76
  87.0 0.5 slice_bitcast_fusion.1
  87.5 1.1 fusion.11
  88.6 0.2 slice_bitcast_fusion.2
  88.7 1.9 %collective-permute-start.3 = (bf16[384,384]{0,1:T(8,128)(2,1)S(1)}, bf16[384,384]{0,1:T(8,128)(2,1)S(1)}, u32[]{:S(2)}, u32[]{:S(2)}) collective-permute-start(bf16[384,384]{0,1:T(8,128)(2,1)S(1)} %get-tuple-element.11), channel_id=1, source_target_pairs={{0,1},{1,2},{2,3},{3,4},{4,5},{5,6},{6,7},{7,8},{8,9},{9,10},{10,1... | collective-permute-start | bytes 884744 | tf_op jit(solution)/shard_map/ppermute | solution.py:38
  90.7 4.7 %collective-permute-start.4 = (bf16[384,384]{0,1:T(8,128)(2,1)S(1)}, bf16[384,384]{0,1:T(8,128)(2,1)S(1)}, u32[]{:S(2)}, u32[]{:S(2)}) collective-permute-start(bf16[384,384]{0,1:T(8,128)(2,1)S(1)} %get-tuple-element.10), channel_id=1, source_target_pairs={{0,1},{1,2},{2,3},{3,4},{4,5},{5,6},{6,7},{7,8},{8,9},{9,10},{10,1... | collective-permute-start | bytes 884744 | tf_op jit(solution)/shard_map/ppermute | solution.py:38
  95.4 3.3 %collective-permute-start.5 = (bf16[384,384]{0,1:T(8,128)(2,1)S(1)}, bf16[384,384]{0,1:T(8,128)(2,1)S(1)}, u32[]{:S(2)}, u32[]{:S(2)}) collective-permute-start(bf16[384,384]{0,1:T(8,128)(2,1)S(1)} %get-tuple-element.9), channel_id=1, source_target_pairs={{0,1},{1,2},{2,3},{3,4},{4,5},{5,6},{6,7},{7,8},{8,9},{9,10},{10,1... | collective-permute-start | bytes 884744 | tf_op jit(solution)/shard_map/ppermute | solution.py:38
  98.7 3.4 %collective-permute-start.6 = (bf16[384,384]{0,1:T(8,128)(2,1)S(1)}, bf16[384,384]{0,1:T(8,128)(2,1)S(1)}, u32[]{:S(2)}, u32[]{:S(2)}) collective-permute-start(bf16[384,384]{0,1:T(8,128)(2,1)S(1)} %get-tuple-element.8), channel_id=1, source_target_pairs={{0,1},{1,2},{2,3},{3,4},{4,5},{5,6},{6,7},{7,8},{8,9},{9,10},{10,1... | collective-permute-start | bytes 884744 | tf_op jit(solution)/shard_map/ppermute | solution.py:38
  102.1 1.9 %collective-permute-start.7 = (bf16[384,384]{0,1:T(8,128)(2,1)S(1)}, bf16[384,384]{0,1:T(8,128)(2,1)S(1)}, u32[]{:S(2)}, u32[]{:S(2)}) collective-permute-start(bf16[384,384]{0,1:T(8,128)(2,1)S(1)} %get-tuple-element.7), channel_id=1, source_target_pairs={{0,1},{1,2},{2,3},{3,4},{4,5},{5,6},{6,7},{7,8},{8,9},{9,10},{10,1... | collective-permute-start | bytes 884744 | tf_op jit(solution)/shard_map/ppermute | solution.py:38
  104.0 0.0 collective-permute-done.3
  104.1 0.0 collective-permute-done.4
  104.1 1.7 %collective-permute-done.5 = bf16[384,384]{0,1:T(8,128)(2,1)S(1)} collective-permute-done((bf16[384,384]{0,1:T(8,128)(2,1)S(1)}, bf16[384,384]{0,1:T(8,128)(2,1)S(1)}, u32[]{:S(2)}, u32[]{:S(2)}) %collective-permute-start.5) | collective-permute-done | bytes 294944 | tf_op jit(solution)/shard_map/ppermute | solution.py:38
  105.9 3.3 %collective-permute-done.6 = bf16[384,384]{0,1:T(8,128)(2,1)S(1)} collective-permute-done((bf16[384,384]{0,1:T(8,128)(2,1)S(1)}, bf16[384,384]{0,1:T(8,128)(2,1)S(1)}, u32[]{:S(2)}, u32[]{:S(2)}) %collective-permute-start.6) | collective-permute-done | bytes 294944 | tf_op jit(solution)/shard_map/ppermute | solution.py:38
  109.2 3.4 %collective-permute-done.7 = bf16[384,384]{0,1:T(8,128)(2,1)S(1)} collective-permute-done((bf16[384,384]{0,1:T(8,128)(2,1)S(1)}, bf16[384,384]{0,1:T(8,128)(2,1)S(1)}, u32[]{:S(2)}, u32[]{:S(2)}) %collective-permute-start.7) | collective-permute-done | bytes 294944 | tf_op jit(solution)/shard_map/ppermute | solution.py:38
  112.6 1.2 fusion.14
  113.8 2.2 %copy.9 = bf16[1,5,384,384]{3,2,1,0:T(8,128)(2,1)} copy(bf16[1,5,384,384]{2,3,1,0:T(8,128)(2,1)S(1)} %fusion.14) | data formatting | bytes 2949120 | tf_op jit(solution)/shard_map/broadcast_in_dim | solution.py:87
  (5 shorter events, 0.2 us)
Async XLA Ops:
  0.0 55.2 %copy-start = (bf16[1,2,384,384]{3,2,1,0:T(8,128)(2,1)S(1)}, bf16[1,2,384,384]{3,2,1,0:T(8,128)(2,1)}, u32[]{:S(2)}) copy-start(bf16[1,2,384,384]{3,2,1,0:T(8,128)(2,1)} %param.5) | copy-start | bytes 1769476
  0.0 55.5 %collective-permute-start.2 = (bf16[5,384,384]{2,1,0:T(8,128)(2,1)}, bf16[5,384,384]{2,1,0:T(8,128)(2,1)S(1)}, u32[]{:S(2)}, u32[]{:S(2)}) collective-permute-start(bf16[5,384,384]{2,1,0:T(8,128)(2,1)} %bitcast.72), channel_id=1, source_target_pairs={{0,16},{16,32},{32,48},{48,64},{64,80},{80,96},{96,112},{112,128},... | collective-permute-start | bytes 4423688 | tf_op jit(solution)/shard_map/ppermute | solution.py:16
  4.0 48.0 %collective-permute-start = (bf16[2,384,384]{2,1,0:T(8,128)(2,1)}, bf16[2,384,384]{2,1,0:T(8,128)(2,1)S(1)}, u32[]{:S(2)}, u32[]{:S(2)}) collective-permute-start(bf16[2,384,384]{2,1,0:T(8,128)(2,1)} %bitcast.70), channel_id=1, source_target_pairs={{1,0},{2,1},{3,2},{4,3},{5,4},{6,5},{7,6},{8,7},{9,8},{10,9},{11,1... | collective-permute-start | bytes 1769480 | tf_op jit(solution)/shard_map/ppermute | solution.py:28
  8.3 46.8 %collective-permute-start.1 = (bf16[2,384,384]{2,1,0:T(8,128)(2,1)}, bf16[2,384,384]{2,1,0:T(8,128)(2,1)S(1)}, u32[]{:S(2)}, u32[]{:S(2)}) collective-permute-start(bf16[2,384,384]{2,1,0:T(8,128)(2,1)} %bitcast.71), channel_id=1, source_target_pairs={{0,1},{1,2},{2,3},{3,4},{4,5},{5,6},{6,7},{7,8},{8,9},{9,10},{10,1... | collective-permute-start | bytes 1769480 | tf_op jit(solution)/shard_map/ppermute | solution.py:26
  12.1 43.4 %copy-start.1 = (bf16[5,384,384]{2,1,0:T(8,128)(2,1)S(1)}, bf16[5,384,384]{2,1,0:T(8,128)(2,1)}, u32[]{:S(2)}) copy-start(bf16[5,384,384]{2,1,0:T(8,128)(2,1)} %param.8) | copy-start | bytes 4423684
  88.7 15.3 %collective-permute-start.3 = (bf16[384,384]{0,1:T(8,128)(2,1)S(1)}, bf16[384,384]{0,1:T(8,128)(2,1)S(1)}, u32[]{:S(2)}, u32[]{:S(2)}) collective-permute-start(bf16[384,384]{0,1:T(8,128)(2,1)S(1)} %get-tuple-element.11), channel_id=1, source_target_pairs={{0,1},{1,2},{2,3},{3,4},{4,5},{5,6},{6,7},{7,8},{8,9},{9,10},{10,1... | collective-permute-start | bytes 884744 | tf_op jit(solution)/shard_map/ppermute | solution.py:38
  90.7 13.4 %collective-permute-start.4 = (bf16[384,384]{0,1:T(8,128)(2,1)S(1)}, bf16[384,384]{0,1:T(8,128)(2,1)S(1)}, u32[]{:S(2)}, u32[]{:S(2)}) collective-permute-start(bf16[384,384]{0,1:T(8,128)(2,1)S(1)} %get-tuple-element.10), channel_id=1, source_target_pairs={{0,1},{1,2},{2,3},{3,4},{4,5},{5,6},{6,7},{7,8},{8,9},{9,10},{10,1... | collective-permute-start | bytes 884744 | tf_op jit(solution)/shard_map/ppermute | solution.py:38
  95.4 10.4 %collective-permute-start.5 = (bf16[384,384]{0,1:T(8,128)(2,1)S(1)}, bf16[384,384]{0,1:T(8,128)(2,1)S(1)}, u32[]{:S(2)}, u32[]{:S(2)}) collective-permute-start(bf16[384,384]{0,1:T(8,128)(2,1)S(1)} %get-tuple-element.9), channel_id=1, source_target_pairs={{0,1},{1,2},{2,3},{3,4},{4,5},{5,6},{6,7},{7,8},{8,9},{9,10},{10,1... | collective-permute-start | bytes 884744 | tf_op jit(solution)/shard_map/ppermute | solution.py:38
  98.7 10.4 %collective-permute-start.6 = (bf16[384,384]{0,1:T(8,128)(2,1)S(1)}, bf16[384,384]{0,1:T(8,128)(2,1)S(1)}, u32[]{:S(2)}, u32[]{:S(2)}) collective-permute-start(bf16[384,384]{0,1:T(8,128)(2,1)S(1)} %get-tuple-element.8), channel_id=1, source_target_pairs={{0,1},{1,2},{2,3},{3,4},{4,5},{5,6},{6,7},{7,8},{8,9},{9,10},{10,1... | collective-permute-start | bytes 884744 | tf_op jit(solution)/shard_map/ppermute | solution.py:38
  102.1 10.4 %collective-permute-start.7 = (bf16[384,384]{0,1:T(8,128)(2,1)S(1)}, bf16[384,384]{0,1:T(8,128)(2,1)S(1)}, u32[]{:S(2)}, u32[]{:S(2)}) collective-permute-start(bf16[384,384]{0,1:T(8,128)(2,1)S(1)} %get-tuple-element.7), channel_id=1, source_target_pairs={{0,1},{1,2},{2,3},{3,4},{4,5},{5,6},{6,7},{7,8},{8,9},{9,10},{10,1... | collective-permute-start | bytes 884744 | tf_op jit(solution)/shard_map/ppermute | solution.py:38
where the time goes:
time: 116 us
  waiting for transfers between devices  51.2 us (44%)
  starting transfers between devices  25.5 us (22%)
  matrix products  25.1 us (22%)
  local copies, waits for them, and re-layouts  13.2 us (11%)
    ppermute x1, waiting for transfers between devices, extended(): lax.ppermute(head, axis, [((i + 1) % count, i) for i in range(count)])  39.9 us
    dot_general x1, matrix products, local(): jnp.einsum('wvst,wtac->vsac', couplings, products, precision=lax.Precisio...  17.9 us
    ppermute x5, starting transfers between devices, from_behind(): return lax.ppermute(value, axis, pairs)  15.2 us
    dot_general x1, local copies, waits for them, and re-layouts, local(): jnp.einsum('wab,wtbc->wtac', incoming, own_stack, preferred_element_type=...  8.7 us
    ppermute x5, waiting for transfers between devices, from_behind(): return lax.ppermute(value, axis, pairs)  8.3 us
    dot_general x1, matrix products, local(): jnp.einsum('wab,wtbc->wtac', incoming, own_stack, preferred_element_type=...  4.9 us
    ppermute x1, starting transfers between devices, extended(): lax.ppermute(head, axis, [((i + 1) % count, i) for i in range(count)])  4.27 us
    ppermute x1, starting transfers between devices, shifted(): lax.ppermute(value, axis, [(source, source + steps) for source in range(f...  4.03 us
  transfers between devices with their start and end apart: 8, of which 5 were waited for; matrix products, arithmetic and copies ran while one was open for 2% of the time, Pallas kernels for 0%

commit v1 on v0

v1 whole, which is shorter than its diff:
```python
import jax
import jax.numpy as jnp
from jax import lax
from jax.experimental import pallas as pl
from jax.experimental.pallas import tpu as pltpu
from jax.sharding import PartitionSpec as P


BF16 = jnp.bfloat16
F32 = jnp.float32
AXES = ("site", "sector")
FLAT = (0, 3, 4)
ROWS = 128
VMEM = 24 * 2**20


def dot(a, b):
    return jnp.dot(a, b, preferred_element_type=F32)


def row_blocks(count):
    step = ROWS if count % ROWS == 0 else count
    return [slice(start, start + step) for start in range(0, count, step)]


def coupling(ref, w, v, s, t):
    return ref[w * 20 + v * 4 + s * 2 + t]


def whole():
    return pl.BlockSpec(memory_space=pltpu.VMEM)


def scalars():
    return pl.BlockSpec(memory_space=pltpu.SMEM)


def kernel_call(body, outs, flops, specs, scratch=()):
    return pl.pallas_call(
        body,
        out_shape=[jax.ShapeDtypeStruct(shape, kind) for shape, kind in outs],
        in_specs=specs,
        out_specs=[whole() for _ in outs],
        scratch_shapes=list(scratch),
        cost_estimate=pl.CostEstimate(flops=flops, bytes_accessed=4_000_000, transcendentals=0),
        compiler_params=pltpu.CompilerParams(vmem_limit_bytes=VMEM),
    )


def early(k, bnd, arr, own, near, up, z034, z1, c2, own_t, near_t, y):
    first = lax.axis_index("site") == 0
    e0 = jnp.where(first, bnd[0], arr[0])
    e1 = jnp.where(first, bnd[1], arr[1])
    own_t[0] = own[0].T
    own_t[1] = own[1].T
    near_t[...] = near[1].T
    y[0] = dot(e0, own[0])
    y[1] = dot(e0, own[1])
    y[2] = dot(e1, up[...])
    for r in row_blocks(y.shape[1]):
        for i, v in enumerate(FLAT):
            z034[i, r] = coupling(k, 0, v, 0, 0) * y[0, r]
        c2[r] = coupling(k, 0, 2, 1, 0) * y[0, r]
        z1[r] = coupling(k, 0, 1, 0, 1) * y[1, r] + coupling(k, 1, 1, 0, 0) * y[2, r]


def middle(k, bnd, arr34, arr10, got10, own, own_t, near, near_t, z034_in, z1_in, c2_in,
           z034, c2, m034, out1, y):
    first = lax.axis_index("site") == 0
    e3 = jnp.where(first, bnd[3], arr34[0])
    e4 = jnp.where(first, bnd[4], arr34[1])
    f0 = jnp.where(first, arr10[0], got10[0])
    f1 = jnp.where(first, arr10[1], got10[1])
    y[0] = dot(e3, own[0])
    y[1] = dot(e3, own[1])
    y[2] = dot(e4, own[0])
    y[3] = dot(e4, own[1])
    y[4] = dot(f0, near[1])
    y[5] = dot(f1, own[0])
    y[6] = dot(f1, own[1])
    z1 = []
    m1 = []
    for r in row_blocks(y.shape[1]):
        for i, v in enumerate(FLAT):
            z034[i, r] = (
                z034_in[i, r]
                + coupling(k, 3, v, 0, 0) * y[0, r]
                + coupling(k, 4, v, 0, 0) * y[2, r]
            )
            m034[i, r] = coupling(k, 0, v, 1, 1) * y[4, r] + coupling(k, 1, v, 1, 0) * y[5, r]
        c2[r] = c2_in[r] + coupling(k, 3, 2, 1, 0) * y[0, r] + coupling(k, 4, 2, 1, 0) * y[2, r]
        z1.append(
            (
                z1_in[r] + coupling(k, 3, 1, 0, 1) * y[1, r] + coupling(k, 4, 1, 0, 1) * y[3, r]
            ).astype(BF16)
        )
        m1.append((coupling(k, 1, 1, 1, 1) * y[6, r]).astype(BF16))
    carried = dot(near_t[...], jnp.concatenate(m1, axis=0)).astype(BF16)
    out1[...] = (dot(own_t[0], jnp.concatenate(z1, axis=0)) + carried.astype(F32)).astype(BF16)


def send(k, bnd, arr2, near, own_t, c2_in, c2, y2):
    e2 = jnp.where(lax.axis_index("site") == 0, bnd[2], arr2[0])
    y2[...] = dot(e2, near[1])
    z = (c2_in[...] + coupling(k, 2, 2, 1, 1) * y2[...]).astype(BF16)
    c2[...] = dot(own_t[1], z).astype(BF16)


def late(k, bnd, arr2, near, own_t, z034_in, y2, p0, last):
    e2 = jnp.where(lax.axis_index("site") == 0, bnd[2], arr2[0])
    y = dot(e2, near[0])
    last[...] = dot(own_t[0], (coupling(k, 2, 2, 0, 0) * y).astype(BF16))
    for i, v in enumerate(FLAT):
        z = (z034_in[i] + coupling(k, 2, v, 0, 1) * y2[...]).astype(BF16)
        p0[i] = dot(own_t[0], z)


def join(k, arr34, got34, near, near_t, m034, p0, out1, out, y):
    first = lax.axis_index("site") == 0
    y[0] = dot(jnp.where(first, arr34[0], got34[0]), near[1])
    y[1] = dot(jnp.where(first, arr34[1], got34[1]), near[1])
    out[0, 1] = out1[...]
    for i, v in enumerate(FLAT):
        z = (
            m034[i] + coupling(k, 3, v, 1, 1) * y[0] + coupling(k, 4, v, 1, 1) * y[1]
        ).astype(BF16)
        carried = dot(near_t[...], z).astype(BF16)
        out[0, v] = (p0[i] + carried.astype(F32)).astype(BF16)


def finish(out_in, p0, c2, out, buf, sem):
    buf[...] = (p0[...] + c2[...].astype(F32)).astype(BF16)
    copy = pltpu.make_async_copy(buf, out.at[0, 2], sem)
    copy.start()
    copy.wait()


def local(sites, sectors, site_tensors, environments, mpo, boundary):
    def pairs(move, starts):
        found = []
        for s in starts:
            for q in range(sectors):
                to, r = move(s, q)
                found.append((s * sectors + q, to * sectors + r % sectors))
        return found

    everywhere = range(sites)
    ahead = pairs(lambda s, q: (s, q + 1), everywhere)
    behind = pairs(lambda s, q: (s, q - 1), everywhere)
    inner = pairs(lambda s, q: (s, q + 1), range(1, sites))
    along = pairs(lambda s, q: (s + 1, q) if s + 1 < sites else (0, q + 1), everywhere)
    along_open = pairs(lambda s, q: (s + 1, q), range(sites - 1))

    own = site_tensors[0]
    env = environments[0]
    size = own.shape[-1]
    block = (size, size)
    flop = 2 * size**3
    k = mpo.reshape(-1)
    last = lax.axis_index("site") == sites - 1

    def send_on(value, route):
        return lax.ppermute(value, AXES, route)

    first_piece = jnp.where(last, boundary[0:2], env[0:2])
    arr10 = send_on(first_piece, along)
    near = send_on(own, ahead)
    env_later, _ = lax.optimization_barrier((env, first_piece))
    arr34 = send_on(jnp.where(last, boundary[3:5], env_later[3:5]), along)
    up = send_on(own[0], behind)
    arr2 = send_on(env_later[2:3], along_open)
    got10 = send_on(arr10, inner)

    v = whole()
    z034, z1, c2, own_t, near_t = kernel_call(
        early,
        [((3, *block), F32), (block, F32), (block, F32), ((2, *block), BF16), (block, BF16)],
        3 * flop,
        [scalars()] + [v] * 5,
        [pltpu.VMEM((3, *block), F32)],
    )(k, boundary, arr10, own, near, up)
    got34 = send_on(arr34, inner)
    z034, c2, m034, out1 = kernel_call(
        middle,
        [((3, *block), F32), (block, F32), ((3, *block), F32), (block, BF16)],
        9 * flop,
        [scalars()] + [v] * 11,
        [pltpu.VMEM((7, *block), F32)],
    )(k, boundary, arr34, arr10, got10, own, own_t, near, near_t, z034, z1, c2)
    c2, y2 = kernel_call(
        send, [(block, BF16), (block, F32)], 2 * flop, [scalars()] + [v] * 5
    )(k, boundary, arr2, near, own_t, c2)
    c2 = send_on(c2, ahead)
    p0, tail = kernel_call(
        late, [((3, *block), F32), (block, F32)], 5 * flop, [scalars()] + [v] * 6
    )(k, boundary, arr2, near, own_t, z034, y2)
    (out,) = kernel_call(
        join,
        [((1, 5, *block), BF16)],
        5 * flop,
        [scalars()] + [v] * 7,
        [pltpu.VMEM((2, *block), F32)],
    )(k, arr34, got34, near, near_t, m034, p0, out1)
    (out,) = pl.pallas_call(
        finish,
        out_shape=[jax.ShapeDtypeStruct((1, 5, *block), BF16)],
        in_specs=[pl.BlockSpec(memory_space=pl.ANY), v, v],
        out_specs=[pl.BlockSpec(memory_space=pl.ANY)],
        scratch_shapes=[pltpu.VMEM(block, BF16), pltpu.SemaphoreType.DMA],
        input_output_aliases={0: 0},
        cost_estimate=pl.CostEstimate(flops=size * size, bytes_accessed=1_000_000, transcendentals=0),
        compiler_params=pltpu.CompilerParams(vmem_limit_bytes=VMEM),
        name="finish",
    )(out, tail, c2)
    return out


def solution(mesh):
    in_specs = (
        P("site", None, "sector", None),
        P("site", None, "sector", None),
        P("site", None, None, None, None),
        P(None, "sector", None),
    )

    def body(*args):
        return local(mesh.shape["site"], mesh.shape["sector"], *args)

    return jax.shard_map(
        body, mesh=mesh, in_specs=in_specs, out_specs=P("site", None, "sector", None), check_vma=False
    )
```

time: 116 us -> 69.8 us (0.60)
  matrix products: 25.1 us -> 0 us
  waiting for transfers between devices: 51.2 us -> 29 us
  Pallas kernels: 0 us -> 12.4 us
  local copies, waits for them, and re-layouts: 13.2 us -> 4.1 us
  starting transfers between devices: 25.5 us -> 20.4 us
  other arithmetic: 0.73 us -> 2.6 us
    dot_general x4 -> x0, matrix products: 25.1 us -> none  [the longest x1 17.9 us: local(): jnp.einsum('wvst,wtac->vsac', couplings, products, precision=lax.Precisio...]
    ppermute x8, waiting for transfers between devices: 51.2 us -> 29 us  [send_on(): return lax.ppermute(value, AXES, route)]
    pallas_call x0 -> x6, Pallas kernels: none -> 12.4 us  [the longest x1 3.46 us: local(): kernel_call(join, [((1, 5, *block), BF16)], 5 * flop, [scalars()] + [v] *...]
    dot_general x1 -> x0, local copies, waits for them, and re-layouts: 8.7 us -> none  [local(): jnp.einsum('wab,wtbc->wtac', incoming, own_stack, preferred_element_type=...]
    ppermute x8, starting transfers between devices: 25.5 us -> 20.4 us  [send_on(): return lax.ppermute(value, AXES, route)]
    select_n x0 -> x2, other arithmetic: none -> 2.6 us  [the longest x1 1.46 us: local(): first_piece = jnp.where(last, boundary[0:2], env[0:2])]
    broadcast_in_dim x1 -> x0, local copies, waits for them, and re-layouts: 2.16 us -> none  [local(): return state[None]]
    slice x0 -> x1, local copies, waits for them, and re-layouts: none -> 1.73 us  [local(): arr2 = send_on(env_later[2:3], along_open)]
  transfers between devices with their start and end apart: 8 -> 8, of which waited for: 5 -> 4; matrix products, arithmetic and copies ran while one was open for 2% -> 8% of each run, Pallas kernels for 0% -> 17%
where the time goes in v1:
time: 69.8 us; the launch traced here: 68.7 us
  waiting for transfers between devices  29 us (42%)
  starting transfers between devices  20.4 us (29%)
  Pallas kernels  12.4 us (18%)
  local copies, waits for them, and re-layouts  4.1 us (6%)
  other arithmetic  2.6 us (4%)
    ppermute x8, waiting for transfers between devices, send_on(): return lax.ppermute(value, AXES, route)  29 us
    ppermute x8, starting transfers between devices, send_on(): return lax.ppermute(value, AXES, route)  20.4 us
    pallas_call x1, Pallas kernels, local(): kernel_call(join, [((1, 5, *block), BF16)], 5 * flop, [scalars()] + [v] *...  3.46 us
    pallas_call x1, Pallas kernels, local(): kernel_call(middle, [((3, *block), F32), (block, F32), ((3, *block), F32)...  3.35 us
    pallas_call x1, Pallas kernels, local(): kernel_call(early, [((3, *block), F32), (block, F32), (block, F32), ((2,...  1.88 us
    slice x1, local copies, waits for them, and re-layouts, local(): arr2 = send_on(env_later[2:3], along_open)  1.73 us
    pallas_call x1, Pallas kernels, local(): kernel_call(late, [((3, *block), F32), (block, F32)], 5 * flop, [scalars(...  1.72 us
    select_n x1, other arithmetic, local(): first_piece = jnp.where(last, boundary[0:2], env[0:2])  1.46 us
  transfers between devices with their start and end apart: 8, of which 4 were waited for; matrix products, arithmetic and copies ran while one was open for 8% of the time, Pallas kernels for 17%

profile of v1, /device:TPU:24, one launch (start us, length us, event | category | flops | bytes accessed | tf_op | source)
XLA Modules:
  0.0 68.7 jit_solution(10122021574218548413)
XLA Ops:
  0.0 0.0 copy-start
  0.0 0.0 copy-start.1
  0.0 1.5 %bitcast_select_fusion = bf16[2,384,384]{2,1,0:T(8,128)(2,1)S(1)} fusion(bf16[1,5,384,384]{3,2,1,0:T(8,128)(2,1)} %param.5, bf16[5,384,384]{2,1,0:T(8,128)(2,1)} %bnd.7, pred[]{:T(512)S(6)} %eq.3), kind=kLoop, calls=%fused_computation | loop fusion | flops 294912 | bytes 1769473 | tf_op jit(solution)/shard_map/jit(_where)/select_n | solution.py:165
  1.5 3.8 %collective-permute-start.3 = (bf16[2,384,384]{2,1,0:T(8,128)(2,1)S(1)}, bf16[2,384,384]{2,1,0:T(8,128)(2,1)}, u32[]{:S(2)}, u32[]{:S(2)}) collective-permute-start(bf16[2,384,384]{2,1,0:T(8,128)(2,1)S(1)} %bitcast_select_fusion), channel_id=1, source_target_pairs={{0,16},{1,17},{2,18},{3,19},{4,20},{5,21},{6,22},{7,23},{8,24},{9,... | collective-permute-start | bytes 1769480 | tf_op jit(solution)/shard_map/ppermute | solution.py:163
  5.3 0.0 copy-done
  5.3 0.0 copy-start.2
  5.3 1.1 %slice_select_fusion = bf16[2,384,384]{2,1,0:T(8,128)(2,1)S(1)} fusion(bf16[5,384,384]{2,1,0:T(8,128)(2,1)} %bitcast.9, bf16[5,384,384]{2,1,0:T(8,128)(2,1)S(1)} %copy-done, pred[]{:T(512)S(6)} %eq.3), kind=kLoop, calls=%fused_computation.1 | loop fusion | flops 294912 | bytes 1769473 | tf_op jit(solution)/shard_map/jit(_where)/select_n | solution.py:169
  6.5 3.8 %collective-permute-start = (bf16[2,384,384]{2,1,0:T(8,128)(2,1)S(1)}, bf16[2,384,384]{2,1,0:T(8,128)(2,1)S(1)}, u32[]{:S(2)}, u32[]{:S(2)}) collective-permute-start(bf16[2,384,384]{2,1,0:T(8,128)(2,1)S(1)} %slice_select_fusion), channel_id=1, source_target_pairs={{0,16},{1,17},{2,18},{3,19},{4,20},{5,21},{6,22},{7,23},{8,24},{9,... | collective-permute-start | bytes 1769480 | tf_op jit(solution)/shard_map/ppermute | solution.py:163
  10.3 0.0 copy-done.1
  10.3 1.9 %collective-permute-start.2 = (bf16[2,384,384]{2,1,0:T(8,128)(2,1)S(1)}, bf16[2,384,384]{2,1,0:T(8,128)(2,1)S(1)}, u32[]{:S(2)}, u32[]{:S(2)}) collective-permute-start(bf16[2,384,384]{2,1,0:T(8,128)(2,1)S(1)} %bitcast.6), channel_id=1, source_target_pairs={{0,1},{1,2},{2,3},{3,4},{4,5},{5,6},{6,7},{7,8},{8,9},{9,10},{10,1... | collective-permute-start | bytes 1769480 | tf_op jit(solution)/shard_map/ppermute | solution.py:163
  12.2 15.6 %collective-permute-done.3.arr.arr10 = bf16[2,384,384]{2,1,0:T(8,128)(2,1)} collective-permute-done((bf16[2,384,384]{2,1,0:T(8,128)(2,1)S(1)}, bf16[2,384,384]{2,1,0:T(8,128)(2,1)}, u32[]{:S(2)}, u32[]{:S(2)}) %collective-permute-start.3) | collective-permute-done | bytes 589856 | tf_op jit(solution)/shard_map/ppermute | solution.py:163
  27.8 1.5 %collective-permute-start.5 = (bf16[2,384,384]{2,1,0:T(8,128)(2,1)}, bf16[2,384,384]{2,1,0:T(8,128)(2,1)}, u32[]{:S(2)}, u32[]{:S(2)}) collective-permute-start(bf16[2,384,384]{2,1,0:T(8,128)(2,1)} %collective-permute-done.3.arr.arr10), channel_id=1, source_target_pairs={{16,17},{17,18},{18,19},{19,20},{20,21},{21,22},{22,23},{23,24},{2... | collective-permute-start | bytes 1769480 | tf_op jit(solution)/shard_map/ppermute | solution.py:163
  29.3 0.7 %slice_bitcast_fusion = bf16[384,384]{1,0:T(8,128)(2,1)} fusion(bf16[1,2,384,384]{3,2,1,0:T(8,128)(2,1)S(1)} %copy-done.1), kind=kLoop, calls=%fused_computation.2 | loop fusion | bytes 589824 | tf_op jit(solution)/shard_map/squeeze | solution.py:170
  30.1 4.7 %collective-permute-start.4 = (bf16[384,384]{1,0:T(8,128)(2,1)}, bf16[384,384]{1,0:T(8,128)(2,1)}, u32[]{:S(2)}, u32[]{:S(2)}) collective-permute-start(bf16[384,384]{1,0:T(8,128)(2,1)} %slice_bitcast_fusion), channel_id=1, source_target_pairs={{0,15},{1,0},{2,1},{3,2},{4,3},{5,4},{6,5},{7,6},{8,7},{9,8},{10,9... | collective-permute-start | bytes 884744 | tf_op jit(solution)/shard_map/ppermute | solution.py:163
  34.7 5.6 %collective-permute-done.arr34 = bf16[2,384,384]{2,1,0:T(8,128)(2,1)S(1)} collective-permute-done((bf16[2,384,384]{2,1,0:T(8,128)(2,1)S(1)}, bf16[2,384,384]{2,1,0:T(8,128)(2,1)S(1)}, u32[]{:S(2)}, u32[]{:S(2)}) %collective-permute-start) | collective-permute-done | bytes 589856 | tf_op jit(solution)/shard_map/ppermute | solution.py:163
  40.4 1.5 %collective-permute-start.1 = (bf16[2,384,384]{2,1,0:T(8,128)(2,1)S(1)}, bf16[2,384,384]{2,1,0:T(8,128)(2,1)}, u32[]{:S(2)}, u32[]{:S(2)}) collective-permute-start(bf16[2,384,384]{2,1,0:T(8,128)(2,1)S(1)} %collective-permute-done.arr34), channel_id=1, source_target_pairs={{16,17},{17,18},{18,19},{19,20},{20,21},{21,22},{22,23},{23,24},{2... | collective-permute-start | bytes 1769480 | tf_op jit(solution)/shard_map/ppermute | solution.py:163
  41.8 1.7 %slice.28 = bf16[1,384,384]{2,1,0:T(8,128)(2,1)} slice(bf16[5,384,384]{2,1,0:T(8,128)(2,1)} %bitcast.10), slice={[2:3], [0:384], [0:384]} | slice | bytes 589824 | tf_op jit(solution)/shard_map/slice | solution.py:171
  43.6 1.3 %collective-permute-start.6 = (bf16[1,384,384]{2,1,0:T(8,128)(2,1)}, bf16[1,384,384]{2,1,0:T(8,128)(2,1)S(1)}, u32[]{:S(2)}, u32[]{:S(2)}) collective-permute-start(bf16[1,384,384]{2,1,0:T(8,128)(2,1)} %slice.28), channel_id=1, source_target_pairs={{0,16},{1,17},{2,18},{3,19},{4,20},{5,21},{6,22},{7,23},{8,24},{9,... | collective-permute-start | bytes 884744 | tf_op jit(solution)/shard_map/ppermute | solution.py:163
  44.9 0.0 copy-done.2
  44.9 0.7 %copy.7 = f32[1,5,5,2,2]{4,3,2,1,0:T(2,128)} copy(f32[1,5,5,2,2]{2,4,3,1,0:T(2,128)S(1)} %copy-done.2) | data formatting | bytes 800 | tf_op args[2]
  45.6 0.9 %reshape.6.k = f32[100]{0:T(128)S(1)} reshape(f32[1,5,5,2,2]{4,3,2,1,0:T(2,128)} %copy.7) | data formatting | bytes 800 | tf_op jit(solution)/shard_map/reshape | solution.py:159
  46.5 0.0 collective-permute-done.4.up
  46.5 4.5 %collective-permute-done.2.near = bf16[2,384,384]{2,1,0:T(8,128)(2,1)S(1)} collective-permute-done((bf16[2,384,384]{2,1,0:T(8,128)(2,1)S(1)}, bf16[2,384,384]{2,1,0:T(8,128)(2,1)S(1)}, u32[]{:S(2)}, u32[]{:S(2)}) %collective-permute-start.2) | collective-permute-done | bytes 589856 | tf_op jit(solution)/shard_map/ppermute | solution.py:163
  51.0 1.9 %shard_map.46 = (f32[3,384,384]{2,1,0:T(8,128)S(1)}, f32[384,384]{1,0:T(8,128)S(1)}, f32[384,384]{1,0:T(8,128)S(1)}, bf16[2,384,384]{2,1,0:T(8,128)(2,1)S(1)}, bf16[384,384]{1,0:T(8,128)(2,1)S(1)}) custom-call(f32[100]{0:T(128)S(1)} %reshape.6.k, bf16[5,384,384]{2,1,0:T(8,128)(2,1)S(1)} %copy-done, bf16[2,384,384]{2,1,0:T(8,128)(2,1)} %collective-permute-done.3.arr.arr10, ...), custom_call_target="tpu_custom_call" | custom-call | flops 339738624 | bytes 4000000 | tf_op jit(solution)/shard_map/pallas_call | solution.py:175
  52.8 0.0 collective-permute-done.5.got10
  52.9 3.4 %shard_map.47 = (f32[3,384,384]{2,1,0:T(8,128)S(1)}, f32[384,384]{1,0:T(8,128)S(1)}, f32[3,384,384]{2,1,0:T(8,128)S(1)}, bf16[384,384]{1,0:T(8,128)(2,1)S(1)}) custom-call(f32[100]{0:T(128)S(1)} %reshape.6.k, bf16[5,384,384]{2,1,0:T(8,128)(2,1)S(1)} %copy-done, bf16[2,384,384]{2,1,0:T(8,128)(2,1)S(1)} %collective-permute-done.arr34, ...), custom_call_target="tpu_custom_call" | custom-call | flops 1019215872 | bytes 4000000 | tf_op jit(solution)/shard_map/pallas_call | solution.py:183
  56.2 0.0 collective-permute-done.6.arr2
  56.2 1.2 %shard_map.48 = (bf16[384,384]{1,0:T(8,128)(2,1)S(1)}, f32[384,384]{1,0:T(8,128)S(1)}) custom-call(f32[100]{0:T(128)S(1)} %reshape.6.k, bf16[5,384,384]{2,1,0:T(8,128)(2,1)S(1)} %copy-done, bf16[1,384,384]{2,1,0:T(8,128)(2,1)S(1)} %collective-permute-done.6.arr2, bf16[2,384,384]{2,1,0:T(8,128)(2,1)S(1)} %collective-permute-done.2.near, ...), custom_call_target="tpu_custom_call" | custom-call | flops 226492416 | bytes 4000000 | tf_op jit(solution)/shard_map/pallas_call | solution.py:190
  57.4 1.9 %collective-permute-start.7 = (bf16[384,384]{1,0:T(8,128)(2,1)S(1)}, bf16[384,384]{1,0:T(8,128)(2,1)S(1)}, u32[]{:S(2)}, u32[]{:S(2)}) collective-permute-start(bf16[384,384]{1,0:T(8,128)(2,1)S(1)} %get-tuple-element.32), channel_id=1, source_target_pairs={{0,1},{1,2},{2,3},{3,4},{4,5},{5,6},{6,7},{7,8},{8,9},{9,10},{10,1... | collective-permute-start | bytes 884744 | tf_op jit(solution)/shard_map/ppermute | solution.py:163
  59.4 1.7 %shard_map.49 = (f32[3,384,384]{2,1,0:T(8,128)S(1)}, f32[384,384]{1,0:T(8,128)S(1)}) custom-call(f32[100]{0:T(128)S(1)} %reshape.6.k, bf16[5,384,384]{2,1,0:T(8,128)(2,1)S(1)} %copy-done, bf16[1,384,384]{2,1,0:T(8,128)(2,1)S(1)} %collective-permute-done.6.arr2, bf16[2,384,384]{2,1,0:T(8,128)(2,1)S(1)} %collective-permute-done.2.near, ...), custom_call_target="tpu_custom_call" | custom-call | flops 566231040 | bytes 4000000 | tf_op jit(solution)/shard_map/pallas_call | solution.py:194
  61.1 0.0 collective-permute-done.1.got34
  61.1 3.5 %shard_map.50.out_in = bf16[1,5,384,384]{3,2,1,0:T(8,128)(2,1)} custom-call(f32[100]{0:T(128)S(1)} %reshape.6.k, bf16[2,384,384]{2,1,0:T(8,128)(2,1)S(1)} %collective-permute-done.arr34, bf16[2,384,384]{2,1,0:T(8,128)(2,1)} %collective-permute-done.1.got34, bf16[2,384,384]{2,1,0:T(8,128)(2,1)S(1)} %collective-permute-done.2.near, ...), custom_call_target="tpu_custom_call" | custom-call | flops 566231040 | bytes 4000000 | tf_op jit(solution)/shard_map/pallas_call | solution.py:197
  64.6 3.3 %collective-permute-done.7.c2 = bf16[384,384]{1,0:T(8,128)(2,1)S(1)} collective-permute-done((bf16[384,384]{1,0:T(8,128)(2,1)S(1)}, bf16[384,384]{1,0:T(8,128)(2,1)S(1)}, u32[]{:S(2)}, u32[]{:S(2)}) %collective-permute-start.7) | collective-permute-done | bytes 294944 | tf_op jit(solution)/shard_map/ppermute | solution.py:163
  67.9 0.8 %finish.1 = bf16[1,5,384,384]{3,2,1,0:T(8,128)(2,1)} custom-call(bf16[1,5,384,384]{3,2,1,0:T(8,128)(2,1)} %shard_map.50.out_in, f32[384,384]{1,0:T(8,128)S(1)} %get-tuple-element.31.p0, bf16[384,384]{1,0:T(8,128)(2,1)S(1)} %collective-permute-done.7.c2), custom_call_target="tpu_custom_call", output_to_operand_aliasing={{}: (0, {})} | custom-call | flops 147456 | bytes 1000000 | tf_op jit(solution)/shard_map/finish/pallas_call | solution.py:204
Async XLA Ops:
  0.0 5.3 %copy-start = (bf16[5,384,384]{2,1,0:T(8,128)(2,1)S(1)}, bf16[5,384,384]{2,1,0:T(8,128)(2,1)}, u32[]{:S(2)}) copy-start(bf16[5,384,384]{2,1,0:T(8,128)(2,1)} %bnd.7) | copy-start | bytes 4423684
  0.0 10.3 %copy-start.1 = (bf16[1,2,384,384]{3,2,1,0:T(8,128)(2,1)S(1)}, bf16[1,2,384,384]{3,2,1,0:T(8,128)(2,1)}, u32[]{:S(2)}) copy-start(bf16[1,2,384,384]{3,2,1,0:T(8,128)(2,1)} %param.4) | copy-start | bytes 1769476
  1.5 26.3 %collective-permute-start.3 = (bf16[2,384,384]{2,1,0:T(8,128)(2,1)S(1)}, bf16[2,384,384]{2,1,0:T(8,128)(2,1)}, u32[]{:S(2)}, u32[]{:S(2)}) collective-permute-start(bf16[2,384,384]{2,1,0:T(8,128)(2,1)S(1)} %bitcast_select_fusion), channel_id=1, source_target_pairs={{0,16},{1,17},{2,18},{3,19},{4,20},{5,21},{6,22},{7,23},{8,24},{9,... | collective-permute-start | bytes 1769480 | tf_op jit(solution)/shard_map/ppermute | solution.py:163
  5.3 39.6 %copy-start.2 = (f32[1,5,5,2,2]{2,4,3,1,0:T(2,128)S(1)}, f32[1,5,5,2,2]{2,4,3,1,0:T(2,128)}, u32[]{:S(2)}) copy-start(f32[1,5,5,2,2]{2,4,3,1,0:T(2,128)} %param.6) | copy-start | bytes 1204
  6.5 33.9 %collective-permute-start = (bf16[2,384,384]{2,1,0:T(8,128)(2,1)S(1)}, bf16[2,384,384]{2,1,0:T(8,128)(2,1)S(1)}, u32[]{:S(2)}, u32[]{:S(2)}) collective-permute-start(bf16[2,384,384]{2,1,0:T(8,128)(2,1)S(1)} %slice_select_fusion), channel_id=1, source_target_pairs={{0,16},{1,17},{2,18},{3,19},{4,20},{5,21},{6,22},{7,23},{8,24},{9,... | collective-permute-start | bytes 1769480 | tf_op jit(solution)/shard_map/ppermute | solution.py:163
  10.3 40.6 %collective-permute-start.2 = (bf16[2,384,384]{2,1,0:T(8,128)(2,1)S(1)}, bf16[2,384,384]{2,1,0:T(8,128)(2,1)S(1)}, u32[]{:S(2)}, u32[]{:S(2)}) collective-permute-start(bf16[2,384,384]{2,1,0:T(8,128)(2,1)S(1)} %bitcast.6), channel_id=1, source_target_pairs={{0,1},{1,2},{2,3},{3,4},{4,5},{5,6},{6,7},{7,8},{8,9},{9,10},{10,1... | collective-permute-start | bytes 1769480 | tf_op jit(solution)/shard_map/ppermute | solution.py:163
  27.8 25.0 %collective-permute-start.5 = (bf16[2,384,384]{2,1,0:T(8,128)(2,1)}, bf16[2,384,384]{2,1,0:T(8,128)(2,1)}, u32[]{:S(2)}, u32[]{:S(2)}) collective-permute-start(bf16[2,384,384]{2,1,0:T(8,128)(2,1)} %collective-permute-done.3.arr.arr10), channel_id=1, source_target_pairs={{16,17},{17,18},{18,19},{19,20},{20,21},{21,22},{22,23},{23,24},{2... | collective-permute-start | bytes 1769480 | tf_op jit(solution)/shard_map/ppermute | solution.py:163
  30.1 16.4 %collective-permute-start.4 = (bf16[384,384]{1,0:T(8,128)(2,1)}, bf16[384,384]{1,0:T(8,128)(2,1)}, u32[]{:S(2)}, u32[]{:S(2)}) collective-permute-start(bf16[384,384]{1,0:T(8,128)(2,1)} %slice_bitcast_fusion), channel_id=1, source_target_pairs={{0,15},{1,0},{2,1},{3,2},{4,3},{5,4},{6,5},{7,6},{8,7},{9,8},{10,9... | collective-permute-start | bytes 884744 | tf_op jit(solution)/shard_map/ppermute | solution.py:163
  40.4 20.7 %collective-permute-start.1 = (bf16[2,384,384]{2,1,0:T(8,128)(2,1)S(1)}, bf16[2,384,384]{2,1,0:T(8,128)(2,1)}, u32[]{:S(2)}, u32[]{:S(2)}) collective-permute-start(bf16[2,384,384]{2,1,0:T(8,128)(2,1)S(1)} %collective-permute-done.arr34), channel_id=1, source_target_pairs={{16,17},{17,18},{18,19},{19,20},{20,21},{21,22},{22,23},{23,24},{2... | collective-permute-start | bytes 1769480 | tf_op jit(solution)/shard_map/ppermute | solution.py:163
  43.6 12.7 %collective-permute-start.6 = (bf16[1,384,384]{2,1,0:T(8,128)(2,1)}, bf16[1,384,384]{2,1,0:T(8,128)(2,1)S(1)}, u32[]{:S(2)}, u32[]{:S(2)}) collective-permute-start(bf16[1,384,384]{2,1,0:T(8,128)(2,1)} %slice.28), channel_id=1, source_target_pairs={{0,16},{1,17},{2,18},{3,19},{4,20},{5,21},{6,22},{7,23},{8,24},{9,... | collective-permute-start | bytes 884744 | tf_op jit(solution)/shard_map/ppermute | solution.py:163
  57.4 10.4 %collective-permute-start.7 = (bf16[384,384]{1,0:T(8,128)(2,1)S(1)}, bf16[384,384]{1,0:T(8,128)(2,1)S(1)}, u32[]{:S(2)}, u32[]{:S(2)}) collective-permute-start(bf16[384,384]{1,0:T(8,128)(2,1)S(1)} %get-tuple-element.32), channel_id=1, source_target_pairs={{0,1},{1,2},{2,3},{3,4},{4,5},{5,6},{6,7},{7,8},{8,9},{9,10},{10,1... | collective-permute-start | bytes 884744 | tf_op jit(solution)/shard_map/ppermute | solution.py:163

commit v2 on v1

--- a/solution.py
+++ b/solution.py
@@ -47,25 +47,30 @@
     )
 
 
-def early(k, bnd, arr, own, near, up, z034, z1, c2, own_t, near_t, y):
+def split(env, bnd, own, s34, s2, own_up):
+    s34[...] = jnp.where(
+        lax.axis_index("site") == lax.axis_size("site") - 1, bnd[3:5], env[3:5]
+    )
+    s2[...] = env[2:3]
+    own_up[...] = own[0]
+
+
+def early(k, bnd, arr, own, z034, z1, c2, own_t, y):
     first = lax.axis_index("site") == 0
     e0 = jnp.where(first, bnd[0], arr[0])
-    e1 = jnp.where(first, bnd[1], arr[1])
     own_t[0] = own[0].T
     own_t[1] = own[1].T
-    near_t[...] = near[1].T
     y[0] = dot(e0, own[0])
     y[1] = dot(e0, own[1])
-    y[2] = dot(e1, up[...])
     for r in row_blocks(y.shape[1]):
         for i, v in enumerate(FLAT):
             z034[i, r] = coupling(k, 0, v, 0, 0) * y[0, r]
         c2[r] = coupling(k, 0, 2, 1, 0) * y[0, r]
-        z1[r] = coupling(k, 0, 1, 0, 1) * y[1, r] + coupling(k, 1, 1, 0, 0) * y[2, r]
-
-
-def middle(k, bnd, arr34, arr10, got10, own, own_t, near, near_t, z034_in, z1_in, c2_in,
-           z034, c2, m034, out1, y):
+        z1[r] = coupling(k, 0, 1, 0, 1) * y[1, r]
+
+
+def middle(k, bnd, arr34, arr10, got10, own, near, z034_in, z1_in, c2_in,
+           z034, z1, c2, m034, carried1, near_t, y):
     first = lax.axis_index("site") == 0
     e3 = jnp.where(first, bnd[3], arr34[0])
     e4 = jnp.where(first, bnd[4], arr34[1])
@@ -78,8 +83,8 @@
     y[4] = dot(f0, near[1])
     y[5] = dot(f1, own[0])
     y[6] = dot(f1, own[1])
-    z1 = []
     m1 = []
+    near_t[...] = near[1].T
     for r in row_blocks(y.shape[1]):
         for i, v in enumerate(FLAT):
             z034[i, r] = (
@@ -89,14 +94,9 @@
             )
             m034[i, r] = coupling(k, 0, v, 1, 1) * y[4, r] + coupling(k, 1, v, 1, 0) * y[5, r]
         c2[r] = c2_in[r] + coupling(k, 3, 2, 1, 0) * y[0, r] + coupling(k, 4, 2, 1, 0) * y[2, r]
-        z1.append(
-            (
-                z1_in[r] + coupling(k, 3, 1, 0, 1) * y[1, r] + coupling(k, 4, 1, 0, 1) * y[3, r]
-            ).astype(BF16)
-        )
+        z1[r] = z1_in[r] + coupling(k, 3, 1, 0, 1) * y[1, r] + coupling(k, 4, 1, 0, 1) * y[3, r]
         m1.append((coupling(k, 1, 1, 1, 1) * y[6, r]).astype(BF16))
-    carried = dot(near_t[...], jnp.concatenate(m1, axis=0)).astype(BF16)
-    out1[...] = (dot(own_t[0], jnp.concatenate(z1, axis=0)) + carried.astype(F32)).astype(BF16)
+    carried1[...] = dot(near_t[...], jnp.concatenate(m1, axis=0)).astype(BF16)
 
 
 def send(k, bnd, arr2, near, own_t, c2_in, c2, y2):
@@ -106,13 +106,17 @@
     c2[...] = dot(own_t[1], z).astype(BF16)
 
 
-def late(k, bnd, arr2, near, own_t, z034_in, y2, p0, last):
+def late(k, bnd, arr2, arr10, near, up, own_t, z034_in, z1_in, carried1, y2, p0, last, out1):
     e2 = jnp.where(lax.axis_index("site") == 0, bnd[2], arr2[0])
     y = dot(e2, near[0])
     last[...] = dot(own_t[0], (coupling(k, 2, 2, 0, 0) * y).astype(BF16))
     for i, v in enumerate(FLAT):
         z = (z034_in[i] + coupling(k, 2, v, 0, 1) * y2[...]).astype(BF16)
         p0[i] = dot(own_t[0], z)
+    e1 = jnp.where(lax.axis_index("site") == 0, bnd[1], arr10[1])
+    y = dot(e1, up[...])
+    z = (z1_in[...] + coupling(k, 1, 1, 0, 0) * y).astype(BF16)
+    out1[...] = (dot(own_t[0], z) + carried1[...].astype(F32)).astype(BF16)
 
 
 def join(k, arr34, got34, near, near_t, m034, p0, out1, out, y):
@@ -162,38 +166,46 @@
     def send_on(value, route):
         return lax.ppermute(value, AXES, route)
 
-    first_piece = jnp.where(last, boundary[0:2], env[0:2])
-    arr10 = send_on(first_piece, along)
+    v = whole()
+    arr10 = send_on(jnp.where(last, boundary[0:2], env[0:2]), along)
+    s34, s2, own_up = kernel_call(
+        split, [((2, *block), BF16), ((1, *block), BF16), (block, BF16)], size * size, [v] * 3
+    )(env, boundary, own)
     near = send_on(own, ahead)
-    env_later, _ = lax.optimization_barrier((env, first_piece))
-    arr34 = send_on(jnp.where(last, boundary[3:5], env_later[3:5]), along)
-    up = send_on(own[0], behind)
-    arr2 = send_on(env_later[2:3], along_open)
+    arr34 = send_on(s34, along)
+    up = send_on(own_up, behind)
+    arr2 = send_on(s2, along_open)
     got10 = send_on(arr10, inner)
 
-    v = whole()
-    z034, z1, c2, own_t, near_t = kernel_call(
+    z034, z1, c2, own_t = kernel_call(
         early,
-        [((3, *block), F32), (block, F32), (block, F32), ((2, *block), BF16), (block, BF16)],
-        3 * flop,
-        [scalars()] + [v] * 5,
-        [pltpu.VMEM((3, *block), F32)],
-    )(k, boundary, arr10, own, near, up)
+        [((3, *block), F32), (block, F32), (block, F32), ((2, *block), BF16)],
+        2 * flop,
+        [scalars()] + [v] * 3,
+        [pltpu.VMEM((2, *block), F32)],
+    )(k, boundary, arr10, own)
     got34 = send_on(arr34, inner)
-    z034, c2, m034, out1 = kernel_call(
+    z034, z1, c2, m034, carried1, near_t = kernel_call(
         middle,
-        [((3, *block), F32), (block, F32), ((3, *block), F32), (block, BF16)],
-        9 * flop,
-        [scalars()] + [v] * 11,
+        [
+            ((3, *block), F32),
+            (block, F32),
+            (block, F32),
+            ((3, *block), F32),
+            (block, BF16),
+            (block, BF16),
+        ],
+        8 * flop,
+        [scalars()] + [v] * 9,
         [pltpu.VMEM((7, *block), F32)],
-    )(k, boundary, arr34, arr10, got10, own, own_t, near, near_t, z034, z1, c2)
+    )(k, boundary, arr34, arr10, got10, own, near, z034, z1, c2)
     c2, y2 = kernel_call(
         send, [(block, BF16), (block, F32)], 2 * flop, [scalars()] + [v] * 5
     )(k, boundary, arr2, near, own_t, c2)
     c2 = send_on(c2, ahead)
-    p0, tail = kernel_call(
-        late, [((3, *block), F32), (block, F32)], 5 * flop, [scalars()] + [v] * 6
-    )(k, boundary, arr2, near, own_t, z034, y2)
+    p0, tail, out1 = kernel_call(
+        late, [((3, *block), F32), (block, F32), (block, BF16)], 7 * flop, [scalars()] + [v] * 10
+    )(k, boundary, arr2, arr10, near, up, own_t, z034, z1, carried1, y2)
     (out,) = kernel_call(
         join,
         [((1, 5, *block), BF16)],

time: 69.8 us -> 70.4 us (level)
  the two profiles are of different devices: /device:TPU:24 before, /device:TPU:2 now
where the time goes in v2:
time: 70.4 us; the launch traced here: 69.8 us
  waiting for transfers between devices  26 us (37%)
  starting transfers between devices  24.5 us (35%)
  Pallas kernels  13.7 us (19%)
  local copies, waits for them, and re-layouts  4.05 us (6%)
  other arithmetic  1.43 us (2%)
    ppermute x8, waiting for transfers between devices, send_on(): return lax.ppermute(value, AXES, route)  26 us
    ppermute x8, starting transfers between devices, send_on(): return lax.ppermute(value, AXES, route)  24.5 us
    pallas_call x1, Pallas kernels, local(): kernel_call(join, [((1, 5, *block), BF16)], 5 * flop, [scalars()] + [v] *...  3.63 us
    pallas_call x1, Pallas kernels, local(): kernel_call(middle, [((3, *block), F32), (block, F32), (block, F32), ((3,...  3.31 us
    unnamed x11, local copies, waits for them, and re-layouts  3.18 us
    pallas_call x1, Pallas kernels, local(): kernel_call(late, [((3, *block), F32), (block, F32), (block, BF16)], 7 *...  2.65 us
    select_n x1, other arithmetic, local(): arr10 = send_on(jnp.where(last, boundary[0:2], env[0:2]), along)  1.43 us
  transfers between devices with their start and end apart: 8, of which 3 were waited for; matrix products, arithmetic and copies ran while one was open for 2% of the time, Pallas kernels for 18%

profile of v2, /device:TPU:2, one launch (start us, length us, event | category | flops | bytes accessed | tf_op | source)
XLA Modules:
  0.0 69.8 jit_solution(4879104675343735323)
XLA Ops:
  0.0 0.0 copy-start
  0.0 1.4 %bitcast_select_fusion = bf16[2,384,384]{2,1,0:T(8,128)(2,1)S(1)} fusion(bf16[1,5,384,384]{3,2,1,0:T(8,128)(2,1)} %param.5, bf16[5,384,384]{2,1,0:T(8,128)(2,1)} %bnd.9, pred[]{:T(512)S(6)} %eq.3), kind=kLoop, calls=%fused_computation | loop fusion | flops 294912 | bytes 1769473 | tf_op jit(solution)/shard_map/jit(_where)/select_n | solution.py:170
  1.4 3.8 %collective-permute-start.3 = (bf16[2,384,384]{2,1,0:T(8,128)(2,1)S(1)}, bf16[2,384,384]{2,1,0:T(8,128)(2,1)S(1)}, u32[]{:S(2)}, u32[]{:S(2)}) collective-permute-start(bf16[2,384,384]{2,1,0:T(8,128)(2,1)S(1)} %bitcast_select_fusion), channel_id=1, source_target_pairs={{0,16},{1,17},{2,18},{3,19},{4,20},{5,21},{6,22},{7,23},{8,24},{9,... | collective-permute-start | bytes 1769480 | tf_op jit(solution)/shard_map/ppermute | solution.py:167
  5.3 0.0 copy-done
  5.3 0.0 copy-start.1
  5.3 1.1 %copy-done.1 = bf16[1,2,384,384]{3,2,1,0:T(8,128)(2,1)S(1)} copy-done((bf16[1,2,384,384]{3,2,1,0:T(8,128)(2,1)S(1)}, bf16[1,2,384,384]{3,2,1,0:T(8,128)(2,1)}, u32[]{:S(2)}) %copy-start.1) | copy-done | bytes 589848
  6.3 0.0 copy-start.3
  6.3 1.4 %copy-done.3 = bf16[1,5,384,384]{3,2,1,0:T(8,128)(2,1)S(1)} copy-done((bf16[1,5,384,384]{3,2,1,0:T(8,128)(2,1)S(1)}, bf16[1,5,384,384]{3,2,1,0:T(8,128)(2,1)}, u32[]{:S(2)}) %copy-start.3) | copy-done | bytes 1474584
  7.7 0.0 copy-start.2
  7.7 0.0 copy-start.4
  7.7 1.0 %shard_map.46 = (bf16[2,384,384]{2,1,0:T(8,128)(2,1)S(1)}, bf16[1,384,384]{2,1,0:T(8,128)(2,1)}, bf16[384,384]{1,0:T(8,128)(2,1)}) custom-call(bf16[5,384,384]{2,1,0:T(8,128)(2,1)S(1)} %bitcast.8, bf16[5,384,384]{2,1,0:T(8,128)(2,1)S(1)} %copy-done, bf16[2,384,384]{2,1,0:T(8,128)(2,1)S(1)} %bitcast.4), custom_call_target="tpu_custom_call" | custom-call | flops 147456 | bytes 4000000 | tf_op jit(solution)/shard_map/pallas_call | solution.py:171
  8.7 3.8 %collective-permute-start = (bf16[2,384,384]{2,1,0:T(8,128)(2,1)S(1)}, bf16[2,384,384]{2,1,0:T(8,128)(2,1)}, u32[]{:S(2)}, u32[]{:S(2)}) collective-permute-start(bf16[2,384,384]{2,1,0:T(8,128)(2,1)S(1)} %get-tuple-element.23), channel_id=1, source_target_pairs={{0,16},{1,17},{2,18},{3,19},{4,20},{5,21},{6,22},{7,23},{8,24},{9,... | collective-permute-start | bytes 1769480 | tf_op jit(solution)/shard_map/ppermute | solution.py:167
  12.5 0.0 copy-done.2
  12.5 1.9 %collective-permute-start.2 = (bf16[2,384,384]{2,1,0:T(8,128)(2,1)S(1)}, bf16[2,384,384]{2,1,0:T(8,128)(2,1)S(1)}, u32[]{:S(2)}, u32[]{:S(2)}) collective-permute-start(bf16[2,384,384]{2,1,0:T(8,128)(2,1)S(1)} %bitcast.5), channel_id=1, source_target_pairs={{0,1},{1,2},{2,3},{3,4},{4,5},{5,6},{6,7},{7,8},{8,9},{9,10},{10,1... | collective-permute-start | bytes 1769480 | tf_op jit(solution)/shard_map/ppermute | solution.py:167
  14.5 12.6 %collective-permute-done.3.arr.arr10 = bf16[2,384,384]{2,1,0:T(8,128)(2,1)S(1)} collective-permute-done((bf16[2,384,384]{2,1,0:T(8,128)(2,1)S(1)}, bf16[2,384,384]{2,1,0:T(8,128)(2,1)S(1)}, u32[]{:S(2)}, u32[]{:S(2)}) %collective-permute-start.3) | collective-permute-done | bytes 589856 | tf_op jit(solution)/shard_map/ppermute | solution.py:167
  27.1 1.9 %collective-permute-start.4 = (bf16[2,384,384]{2,1,0:T(8,128)(2,1)S(1)}, bf16[2,384,384]{2,1,0:T(8,128)(2,1)}, u32[]{:S(2)}, u32[]{:S(2)}) collective-permute-start(bf16[2,384,384]{2,1,0:T(8,128)(2,1)S(1)} %collective-permute-done.3.arr.arr10), channel_id=1, source_target_pairs={{16,17},{17,18},{18,19},{19,20},{20,21},{21,22},{22,23},{23,24},{2... | collective-permute-start | bytes 1769480 | tf_op jit(solution)/shard_map/ppermute | solution.py:167
  29.0 10.0 %collective-permute-done.arr34 = bf16[2,384,384]{2,1,0:T(8,128)(2,1)} collective-permute-done((bf16[2,384,384]{2,1,0:T(8,128)(2,1)S(1)}, bf16[2,384,384]{2,1,0:T(8,128)(2,1)}, u32[]{:S(2)}, u32[]{:S(2)}) %collective-permute-start) | collective-permute-done | bytes 589856 | tf_op jit(solution)/shard_map/ppermute | solution.py:167
  39.0 1.9 %collective-permute-start.1 = (bf16[2,384,384]{2,1,0:T(8,128)(2,1)}, bf16[2,384,384]{2,1,0:T(8,128)(2,1)}, u32[]{:S(2)}, u32[]{:S(2)}) collective-permute-start(bf16[2,384,384]{2,1,0:T(8,128)(2,1)} %collective-permute-done.arr34), channel_id=1, source_target_pairs={{16,17},{17,18},{18,19},{19,20},{20,21},{21,22},{22,23},{23,24},{2... | collective-permute-start | bytes 1769480 | tf_op jit(solution)/shard_map/ppermute | solution.py:167
  40.9 1.9 %collective-permute-start.5 = (bf16[1,384,384]{2,1,0:T(8,128)(2,1)}, bf16[1,384,384]{2,1,0:T(8,128)(2,1)S(1)}, u32[]{:S(2)}, u32[]{:S(2)}) collective-permute-start(bf16[1,384,384]{2,1,0:T(8,128)(2,1)} %get-tuple-element.29), channel_id=1, source_target_pairs={{0,16},{1,17},{2,18},{3,19},{4,20},{5,21},{6,22},{7,23},{8,24},{9,... | collective-permute-start | bytes 884744 | tf_op jit(solution)/shard_map/ppermute | solution.py:167
  42.8 7.3 %collective-permute-start.6 = (bf16[384,384]{1,0:T(8,128)(2,1)}, bf16[384,384]{1,0:T(8,128)(2,1)}, u32[]{:S(2)}, u32[]{:S(2)}) collective-permute-start(bf16[384,384]{1,0:T(8,128)(2,1)} %get-tuple-element.30), channel_id=1, source_target_pairs={{0,15},{1,0},{2,1},{3,2},{4,3},{5,4},{6,5},{7,6},{8,7},{9,8},{10,9... | collective-permute-start | bytes 884744 | tf_op jit(solution)/shard_map/ppermute | solution.py:167
  50.1 0.0 copy-done.4
  50.1 0.7 %copy.7 = f32[1,5,5,2,2]{4,3,2,1,0:T(2,128)} copy(f32[1,5,5,2,2]{2,4,3,1,0:T(2,128)S(1)} %copy-done.4) | data formatting | bytes 800 | tf_op args[2]
  50.8 0.9 %reshape.4.k = f32[100]{0:T(128)S(1)} reshape(f32[1,5,5,2,2]{4,3,2,1,0:T(2,128)} %copy.7) | data formatting | bytes 800 | tf_op jit(solution)/shard_map/reshape | solution.py:163
  51.7 1.1 %shard_map.47 = (f32[3,384,384]{2,1,0:T(8,128)S(1)}, f32[384,384]{1,0:T(8,128)S(1)}, f32[384,384]{1,0:T(8,128)S(1)}, bf16[2,384,384]{2,1,0:T(8,128)(2,1)S(1)}) custom-call(f32[100]{0:T(128)S(1)} %reshape.4.k, bf16[5,384,384]{2,1,0:T(8,128)(2,1)S(1)} %copy-done, bf16[2,384,384]{2,1,0:T(8,128)(2,1)S(1)} %collective-permute-done.3.arr.arr10, ...), custom_call_target="tpu_custom_call" | custom-call | flops 226492416 | bytes 4000000 | tf_op jit(solution)/shard_map/pallas_call | solution.py:180
  52.9 0.0 collective-permute-done.2.near
  52.9 0.0 collective-permute-done.4.got10
  52.9 3.3 %shard_map.48 = (f32[3,384,384]{2,1,0:T(8,128)S(1)}, f32[384,384]{1,0:T(8,128)S(1)}, f32[384,384]{1,0:T(8,128)S(1)}, f32[3,384,384]{2,1,0:T(8,128)S(1)}, bf16[38...) custom-call(f32[100]{0:T(128)S(1)} %reshape.4.k, bf16[5,384,384]{2,1,0:T(8,128)(2,1)S(1)} %copy-done, ...), custom_call_target="tpu_custom_call" | custom-call | flops 905969664 | bytes 4000000 | tf_op jit(solution)/shard_map/pallas_call | solution.py:188
  56.2 0.0 collective-permute-done.5.arr2
  56.2 1.2 %shard_map.49 = (bf16[384,384]{1,0:T(8,128)(2,1)S(1)}, f32[384,384]{1,0:T(8,128)S(1)}) custom-call(f32[100]{0:T(128)S(1)} %reshape.4.k, bf16[5,384,384]{2,1,0:T(8,128)(2,1)S(1)} %copy-done, bf16[1,384,384]{2,1,0:T(8,128)(2,1)S(1)} %collective-permute-done.5.arr2, bf16[2,384,384]{2,1,0:T(8,128)(2,1)S(1)} %collective-permute-done.2.near, ...), custom_call_target="tpu_custom_call" | custom-call | flops 226492416 | bytes 4000000 | tf_op jit(solution)/shard_map/pallas_call | solution.py:202
  57.4 1.9 %collective-permute-start.7 = (bf16[384,384]{1,0:T(8,128)(2,1)S(1)}, bf16[384,384]{1,0:T(8,128)(2,1)S(1)}, u32[]{:S(2)}, u32[]{:S(2)}) collective-permute-start(bf16[384,384]{1,0:T(8,128)(2,1)S(1)} %get-tuple-element.40), channel_id=1, source_target_pairs={{0,1},{1,2},{2,3},{3,4},{4,5},{5,6},{6,7},{7,8},{8,9},{9,10},{10,1... | collective-permute-start | bytes 884744 | tf_op jit(solution)/shard_map/ppermute | solution.py:167
  59.3 0.0 collective-permute-done.6.up
  59.4 2.6 %shard_map.50 = (f32[3,384,384]{2,1,0:T(8,128)S(1)}, f32[384,384]{1,0:T(8,128)S(1)}, bf16[384,384]{1,0:T(8,128)(2,1)S(1)}) custom-call(f32[100]{0:T(128)S(1)} %reshape.4.k, bf16[5,384,384]{2,1,0:T(8,128)(2,1)S(1)} %copy-done, bf16[1,384,384]{2,1,0:T(8,128)(2,1)S(1)} %collective-permute-done.5.arr2, ...), custom_call_target="tpu_custom_call" | custom-call | flops 792723456 | bytes 4000000 | tf_op jit(solution)/shard_map/pallas_call | solution.py:206
  62.0 0.0 collective-permute-done.1.got34
  62.0 3.6 %shard_map.51.out_in = bf16[1,5,384,384]{3,2,1,0:T(8,128)(2,1)} custom-call(f32[100]{0:T(128)S(1)} %reshape.4.k, bf16[2,384,384]{2,1,0:T(8,128)(2,1)} %collective-permute-done.arr34, bf16[2,384,384]{2,1,0:T(8,128)(2,1)} %collective-permute-done.1.got34, bf16[2,384,384]{2,1,0:T(8,128)(2,1)S(1)} %collective-permute-done.2.near, ...), custom_call_target="tpu_custom_call" | custom-call | flops 566231040 | bytes 4000000 | tf_op jit(solution)/shard_map/pallas_call | solution.py:209
  65.6 3.4 %collective-permute-done.7.c2 = bf16[384,384]{1,0:T(8,128)(2,1)S(1)} collective-permute-done((bf16[384,384]{1,0:T(8,128)(2,1)S(1)}, bf16[384,384]{1,0:T(8,128)(2,1)S(1)}, u32[]{:S(2)}, u32[]{:S(2)}) %collective-permute-start.7) | collective-permute-done | bytes 294944 | tf_op jit(solution)/shard_map/ppermute | solution.py:167
  69.1 0.8 %finish.1 = bf16[1,5,384,384]{3,2,1,0:T(8,128)(2,1)} custom-call(bf16[1,5,384,384]{3,2,1,0:T(8,128)(2,1)} %shard_map.51.out_in, f32[384,384]{1,0:T(8,128)S(1)} %get-tuple-element.39.p0, bf16[384,384]{1,0:T(8,128)(2,1)S(1)} %collective-permute-done.7.c2), custom_call_target="tpu_custom_call", output_to_operand_aliasing={{}: (0, {})} | custom-call | flops 147456 | bytes 1000000 | tf_op jit(solution)/shard_map/finish/pallas_call | solution.py:216
Async XLA Ops:
  0.0 5.3 %copy-start = (bf16[5,384,384]{2,1,0:T(8,128)(2,1)S(1)}, bf16[5,384,384]{2,1,0:T(8,128)(2,1)}, u32[]{:S(2)}) copy-start(bf16[5,384,384]{2,1,0:T(8,128)(2,1)} %bnd.9) | copy-start | bytes 4423684
  1.4 25.6 %collective-permute-start.3 = (bf16[2,384,384]{2,1,0:T(8,128)(2,1)S(1)}, bf16[2,384,384]{2,1,0:T(8,128)(2,1)S(1)}, u32[]{:S(2)}, u32[]{:S(2)}) collective-permute-start(bf16[2,384,384]{2,1,0:T(8,128)(2,1)S(1)} %bitcast_select_fusion), channel_id=1, source_target_pairs={{0,16},{1,17},{2,18},{3,19},{4,20},{5,21},{6,22},{7,23},{8,24},{9,... | collective-permute-start | bytes 1769480 | tf_op jit(solution)/shard_map/ppermute | solution.py:167
  5.3 1.1 %copy-start.1 = (bf16[1,2,384,384]{3,2,1,0:T(8,128)(2,1)S(1)}, bf16[1,2,384,384]{3,2,1,0:T(8,128)(2,1)}, u32[]{:S(2)}) copy-start(bf16[1,2,384,384]{3,2,1,0:T(8,128)(2,1)} %param.4) | copy-start | bytes 1769476
  6.3 1.4 %copy-start.3 = (bf16[1,5,384,384]{3,2,1,0:T(8,128)(2,1)S(1)}, bf16[1,5,384,384]{3,2,1,0:T(8,128)(2,1)}, u32[]{:S(2)}) copy-start(bf16[1,5,384,384]{3,2,1,0:T(8,128)(2,1)} %param.5) | copy-start | bytes 4423684
  7.7 4.8 %copy-start.2 = (bf16[1,2,384,384]{3,2,1,0:T(8,128)(2,1)S(1)}, bf16[1,2,384,384]{3,2,1,0:T(8,128)(2,1)}, u32[]{:S(2)}) copy-start(bf16[1,2,384,384]{3,2,1,0:T(8,128)(2,1)} %param.4) | copy-start | bytes 1769476
  7.7 42.4 %copy-start.4 = (f32[1,5,5,2,2]{2,4,3,1,0:T(2,128)S(1)}, f32[1,5,5,2,2]{2,4,3,1,0:T(2,128)}, u32[]{:S(2)}) copy-start(f32[1,5,5,2,2]{2,4,3,1,0:T(2,128)} %param.6) | copy-start | bytes 1204
  8.7 30.3 %collective-permute-start = (bf16[2,384,384]{2,1,0:T(8,128)(2,1)S(1)}, bf16[2,384,384]{2,1,0:T(8,128)(2,1)}, u32[]{:S(2)}, u32[]{:S(2)}) collective-permute-start(bf16[2,384,384]{2,1,0:T(8,128)(2,1)S(1)} %get-tuple-element.23), channel_id=1, source_target_pairs={{0,16},{1,17},{2,18},{3,19},{4,20},{5,21},{6,22},{7,23},{8,24},{9,... | collective-permute-start | bytes 1769480 | tf_op jit(solution)/shard_map/ppermute | solution.py:167
  12.5 40.3 %collective-permute-start.2 = (bf16[2,384,384]{2,1,0:T(8,128)(2,1)S(1)}, bf16[2,384,384]{2,1,0:T(8,128)(2,1)S(1)}, u32[]{:S(2)}, u32[]{:S(2)}) collective-permute-start(bf16[2,384,384]{2,1,0:T(8,128)(2,1)S(1)} %bitcast.5), channel_id=1, source_target_pairs={{0,1},{1,2},{2,3},{3,4},{4,5},{5,6},{6,7},{7,8},{8,9},{9,10},{10,1... | collective-permute-start | bytes 1769480 | tf_op jit(solution)/shard_map/ppermute | solution.py:167
  27.1 25.8 %collective-permute-start.4 = (bf16[2,384,384]{2,1,0:T(8,128)(2,1)S(1)}, bf16[2,384,384]{2,1,0:T(8,128)(2,1)}, u32[]{:S(2)}, u32[]{:S(2)}) collective-permute-start(bf16[2,384,384]{2,1,0:T(8,128)(2,1)S(1)} %collective-permute-done.3.arr.arr10), channel_id=1, source_target_pairs={{16,17},{17,18},{18,19},{19,20},{20,21},{21,22},{22,23},{23,24},{2... | collective-permute-start | bytes 1769480 | tf_op jit(solution)/shard_map/ppermute | solution.py:167
  39.0 23.0 %collective-permute-start.1 = (bf16[2,384,384]{2,1,0:T(8,128)(2,1)}, bf16[2,384,384]{2,1,0:T(8,128)(2,1)}, u32[]{:S(2)}, u32[]{:S(2)}) collective-permute-start(bf16[2,384,384]{2,1,0:T(8,128)(2,1)} %collective-permute-done.arr34), channel_id=1, source_target_pairs={{16,17},{17,18},{18,19},{19,20},{20,21},{21,22},{22,23},{23,24},{2... | collective-permute-start | bytes 1769480 | tf_op jit(solution)/shard_map/ppermute | solution.py:167
  40.9 15.3 %collective-permute-start.5 = (bf16[1,384,384]{2,1,0:T(8,128)(2,1)}, bf16[1,384,384]{2,1,0:T(8,128)(2,1)S(1)}, u32[]{:S(2)}, u32[]{:S(2)}) collective-permute-start(bf16[1,384,384]{2,1,0:T(8,128)(2,1)} %get-tuple-element.29), channel_id=1, source_target_pairs={{0,16},{1,17},{2,18},{3,19},{4,20},{5,21},{6,22},{7,23},{8,24},{9,... | collective-permute-start | bytes 884744 | tf_op jit(solution)/shard_map/ppermute | solution.py:167
  42.8 16.5 %collective-permute-start.6 = (bf16[384,384]{1,0:T(8,128)(2,1)}, bf16[384,384]{1,0:T(8,128)(2,1)}, u32[]{:S(2)}, u32[]{:S(2)}) collective-permute-start(bf16[384,384]{1,0:T(8,128)(2,1)} %get-tuple-element.30), channel_id=1, source_target_pairs={{0,15},{1,0},{2,1},{3,2},{4,3},{5,4},{6,5},{7,6},{8,7},{9,8},{10,9... | collective-permute-start | bytes 884744 | tf_op jit(solution)/shard_map/ppermute | solution.py:167
  57.4 11.7 %collective-permute-start.7 = (bf16[384,384]{1,0:T(8,128)(2,1)S(1)}, bf16[384,384]{1,0:T(8,128)(2,1)S(1)}, u32[]{:S(2)}, u32[]{:S(2)}) collective-permute-start(bf16[384,384]{1,0:T(8,128)(2,1)S(1)} %get-tuple-element.40), channel_id=1, source_target_pairs={{0,1},{1,2},{2,3},{3,4},{4,5},{5,6},{6,7},{7,8},{8,9},{9,10},{10,1... | collective-permute-start | bytes 884744 | tf_op jit(solution)/shard_map/ppermute | solution.py:167

commit v3 on v2

v3 whole, which is shorter than its diff:
```python
import jax
import jax.numpy as jnp
from jax import lax
from jax.experimental import pallas as pl
from jax.experimental.pallas import tpu as pltpu
from jax.sharding import PartitionSpec as P


BF16 = jnp.bfloat16
F32 = jnp.float32
AXES = ("site", "sector")
FLAT = (0, 3, 4)
ROWS = 128
VMEM = 16 * 2**20


def dot(a, b):
    return jnp.dot(a, b, preferred_element_type=F32)


def row_blocks(count):
    step = ROWS if count % ROWS == 0 else count
    return [slice(start, start + step) for start in range(0, count, step)]


def coupling(ref, w, v, s, t):
    return ref[w * 20 + v * 4 + s * 2 + t]


def whole():
    return pl.BlockSpec(memory_space=pltpu.VMEM)


def scalars():
    return pl.BlockSpec(memory_space=pltpu.SMEM)


def kernel_call(body, outs, flops, specs, scratch=(), place=pltpu.VMEM):
    return pl.pallas_call(
        body,
        out_shape=[jax.ShapeDtypeStruct(shape, kind) for shape, kind in outs],
        in_specs=specs,
        out_specs=[pl.BlockSpec(memory_space=place) for _ in outs],
        scratch_shapes=list(scratch),
        cost_estimate=pl.CostEstimate(flops=flops, bytes_accessed=4_000_000, transcendentals=0),
        compiler_params=pltpu.CompilerParams(vmem_limit_bytes=VMEM),
    )


def split(env, bnd, own, s34, s2, own_up):
    s34[...] = jnp.where(
        lax.axis_index("site") == lax.axis_size("site") - 1, bnd[3:5], env[3:5]
    )
    s2[...] = env[2:3]
    own_up[...] = own[0]


def early(k, bnd, arr10, own, e01, h01, z034, c2, own_t, y):
    h01[...] = arr10[...]
    e01[...] = jnp.where(lax.axis_index("site") == 0, bnd[0:2], arr10[...])
    own_t[0] = own[0].T
    own_t[1] = own[1].T
    y[...] = dot(e01[0], own[0])
    for r in row_blocks(y.shape[0]):
        for i, v in enumerate(FLAT):
            z034[i, r] = coupling(k, 0, v, 0, 0) * y[r]
        c2[r] = coupling(k, 0, 2, 1, 0) * y[r]


def middle(k, bnd, arr34, own, near, z034_in, c2_in, z034, c2, near_t, y):
    near_t[...] = near[1].T
    first = lax.axis_index("site") == 0
    y[0] = dot(jnp.where(first, bnd[3], arr34[0]), own[0])
    y[1] = dot(jnp.where(first, bnd[4], arr34[1]), own[0])
    for r in row_blocks(y.shape[1]):
        for i, v in enumerate(FLAT):
            z034[i, r] = (
                z034_in[i, r]
                + coupling(k, 3, v, 0, 0) * y[0, r]
                + coupling(k, 4, v, 0, 0) * y[1, r]
            )
        c2[r] = c2_in[r] + coupling(k, 3, 2, 1, 0) * y[0, r] + coupling(k, 4, 2, 1, 0) * y[1, r]


def send(k, bnd, arr2, near, own_t, c2_in, c2, y2):
    e2 = jnp.where(lax.axis_index("site") == 0, bnd[2], arr2[0])
    y2[...] = dot(e2, near[1])
    z = (c2_in[...] + coupling(k, 2, 2, 1, 1) * y2[...]).astype(BF16)
    c2[...] = dot(own_t[1], z).astype(BF16)


def late(k, bnd, e01, arr34, arr2, own, near, up, own_t, z034_in, y2, p0, last, p1):
    first = lax.axis_index("site") == 0
    e0 = e01[0].astype(F32)
    e3 = jnp.where(first, bnd[3], arr34[0]).astype(F32)
    e4 = jnp.where(first, bnd[4], arr34[1]).astype(F32)
    e034 = (
        coupling(k, 0, 1, 0, 1) * e0 + coupling(k, 3, 1, 0, 1) * e3 + coupling(k, 4, 1, 0, 1) * e4
    ).astype(BF16)
    y = dot(jnp.where(first, bnd[2], arr2[0]), near[0])
    last[...] = dot(own_t[0], (coupling(k, 2, 2, 0, 0) * y).astype(BF16))
    for i, v in enumerate(FLAT):
        z = (z034_in[i] + coupling(k, 2, v, 0, 1) * y2[...]).astype(BF16)
        p0[i] = dot(own_t[0], z)
    y = coupling(k, 1, 1, 0, 0) * dot(e01[1], up[...])
    p1[...] = dot(own_t[0], (dot(e034, own[1]) + y).astype(BF16))


def join(k, h01, got10, arr34, got34, own, near, near_t, p0, p1, out, y, done, sems):
    copies = []

    def store(v, total):
        i = len(copies)
        done[i] = total.astype(BF16)
        copies.append(pltpu.make_async_copy(done.at[i], out.at[0, v], sems.at[i]))
        copies[i].start()

    first = lax.axis_index("site") == 0
    f1 = jnp.where(first, h01[1], got10[1])
    y[0] = dot(jnp.where(first, h01[0], got10[0]), near[1])
    y[1] = dot(f1, own[0])
    carried = dot(near_t[...], (coupling(k, 1, 1, 1, 1) * dot(f1, own[1])).astype(BF16))
    store(1, p1[...] + carried.astype(BF16).astype(F32))
    y[2] = dot(jnp.where(first, arr34[0], got34[0]), near[1])
    y[3] = dot(jnp.where(first, arr34[1], got34[1]), near[1])
    for i, v in enumerate(FLAT):
        z = (
            coupling(k, 0, v, 1, 1) * y[0]
            + coupling(k, 1, v, 1, 0) * y[1]
            + coupling(k, 3, v, 1, 1) * y[2]
            + coupling(k, 4, v, 1, 1) * y[3]
        ).astype(BF16)
        store(v, p0[i] + dot(near_t[...], z).astype(BF16).astype(F32))
    for copy in copies:
        copy.wait()


def finish(out_in, p0, c2, out, buf, sem):
    buf[...] = (p0[...] + c2[...].astype(F32)).astype(BF16)
    copy = pltpu.make_async_copy(buf, out.at[0, 2], sem)
    copy.start()
    copy.wait()


def local(sites, sectors, site_tensors, environments, mpo, boundary):
    def pairs(move, starts):
        found = []
        for s in starts:
            for q in range(sectors):
                to, r = move(s, q)
                found.append((s * sectors + q, to * sectors + r % sectors))
        return found

    everywhere = range(sites)
    ahead = pairs(lambda s, q: (s, q + 1), everywhere)
    behind = pairs(lambda s, q: (s, q - 1), everywhere)
    inner = pairs(lambda s, q: (s, q + 1), range(1, sites))
    along = pairs(lambda s, q: (s + 1, q) if s + 1 < sites else (0, q + 1), everywhere)
    along_open = pairs(lambda s, q: (s + 1, q), range(sites - 1))

    own = site_tensors[0]
    env = environments[0]
    size = own.shape[-1]
    block = (size, size)
    flop = 2 * size**3
    k = mpo.reshape(-1)
    last = lax.axis_index("site") == sites - 1

    def send_on(value, route):
        return lax.ppermute(value, AXES, route)

    v = whole()
    arr10 = send_on(jnp.where(last, boundary[0:2], env[0:2]), along)
    s34, s2, own_up = kernel_call(
        split, [((2, *block), BF16), ((1, *block), BF16), (block, BF16)], size * size, [v] * 3
    )(env, boundary, own)
    near = send_on(own, ahead)
    arr34 = send_on(s34, along)
    up = send_on(own_up, behind)
    arr2 = send_on(s2, along_open)
    got10 = send_on(arr10, inner)

    e01, h01, z034, c2, own_t = kernel_call(
        early,
        [((2, *block), BF16), ((2, *block), BF16), ((3, *block), F32), (block, F32), ((2, *block), BF16)],
        flop,
        [scalars()] + [v] * 3,
        [pltpu.VMEM(block, F32)],
    )(k, boundary, arr10, own)
    got34 = send_on(arr34, inner)
    z034, c2, near_t = kernel_call(
        middle,
        [((3, *block), F32), (block, F32), (block, BF16)],
        2 * flop,
        [scalars()] + [v] * 6,
        [pltpu.VMEM((2, *block), F32)],
    )(k, boundary, arr34, own, near, z034, c2)
    c2, y2 = kernel_call(
        send, [(block, BF16), (block, F32)], 2 * flop, [scalars()] + [v] * 5
    )(k, boundary, arr2, near, own_t, c2)
    c2 = send_on(c2, ahead)
    p0, tail, p1 = kernel_call(
        late, [((3, *block), F32), (block, F32), (block, F32)], 8 * flop, [scalars()] + [v] * 10
    )(k, boundary, e01, arr34, arr2, own, near, up, own_t, z034, y2)
    (out,) = kernel_call(
        join,
        [((1, 5, *block), BF16)],
        9 * flop,
        [scalars()] + [v] * 9,
        [
            pltpu.VMEM((4, *block), F32),
            pltpu.VMEM((4, *block), BF16),
            pltpu.SemaphoreType.DMA((4,)),
        ],
        place=pltpu.HBM,
    )(k, h01, got10, arr34, got34, own, near, near_t, p0, p1)
    (out,) = pl.pallas_call(
        finish,
        out_shape=[jax.ShapeDtypeStruct((1, 5, *block), BF16)],
        in_specs=[pl.BlockSpec(memory_space=pl.ANY), v, v],
        out_specs=[pl.BlockSpec(memory_space=pl.ANY)],
        scratch_shapes=[pltpu.VMEM(block, BF16), pltpu.SemaphoreType.DMA],
        input_output_aliases={0: 0},
        cost_estimate=pl.CostEstimate(flops=size * size, bytes_accessed=1_000_000, transcendentals=0),
        compiler_params=pltpu.CompilerParams(vmem_limit_bytes=VMEM),
        name="finish",
    )(out, tail, c2)
    return out


def solution(mesh):
    in_specs = (
        P("site", None, "sector", None),
        P("site", None, "sector", None),
        P("site", None, None, None, None),
        P(None, "sector", None),
    )

    def body(*args):
        return local(mesh.shape["site"], mesh.shape["sector"], *args)

    return jax.shard_map(
        body, mesh=mesh, in_specs=in_specs, out_specs=P("site", None, "sector", None), check_vma=False
    )
```

time: 70.4 us -> 73.1 us (1.038)
  the two profiles are of different devices: /device:TPU:2 before, /device:TPU:27 now
where the time goes in v3:
time: 73.1 us; the launch traced here: 72.5 us
  starting transfers between devices  31.8 us (44%)
  waiting for transfers between devices  21 us (29%)
  Pallas kernels  12.9 us (18%)
  local copies, waits for them, and re-layouts  5.43 us (7%)
  other arithmetic  1.14 us (2%)
    ppermute x8, starting transfers between devices, send_on(): return lax.ppermute(value, AXES, route)  31.8 us
    ppermute x8, waiting for transfers between devices, send_on(): return lax.ppermute(value, AXES, route)  21 us
    unnamed x13, local copies, waits for them, and re-layouts  4.57 us
    pallas_call x1, Pallas kernels, local(): kernel_call(join, [((1, 5, *block), BF16)], 9 * flop, [scalars()] + [v] *...  4.2 us
    pallas_call x1, Pallas kernels, local(): kernel_call(late, [((3, *block), F32), (block, F32), (block, F32)], 8 * f...  2.77 us
    pallas_call x1, Pallas kernels, local(): kernel_call(early, [((2, *block), BF16), ((2, *block), BF16), ((3, *block...  1.57 us
  transfers between devices with their start and end apart: 8, of which 3 were waited for; matrix products, arithmetic and copies ran while one was open for 4% of the time, Pallas kernels for 15%

profile of v3, /device:TPU:27, one launch (start us, length us, event | category | flops | bytes accessed | tf_op | source)
XLA Modules:
  0.0 72.5 jit_solution(2288240336203420443)
XLA Ops:
  0.0 0.0 copy-start
  0.0 1.4 %copy-done = bf16[5,384,384]{2,1,0:T(8,128)(2,1)S(1)} copy-done((bf16[5,384,384]{2,1,0:T(8,128)(2,1)S(1)}, bf16[5,384,384]{2,1,0:T(8,128)(2,1)}, u32[]{:S(2)}) %copy-start) | copy-done | bytes 1474584
  1.4 0.0 copy-start.2
  1.4 1.1 %copy-done.2 = bf16[1,2,384,384]{3,2,1,0:T(8,128)(2,1)S(1)} copy-done((bf16[1,2,384,384]{3,2,1,0:T(8,128)(2,1)S(1)}, bf16[1,2,384,384]{3,2,1,0:T(8,128)(2,1)}, u32[]{:S(2)}) %copy-start.2) | copy-done | bytes 589848
  2.4 0.0 copy-start.4
  2.4 1.4 %copy-done.4 = bf16[1,5,384,384]{3,2,1,0:T(8,128)(2,1)S(1)} copy-done((bf16[1,5,384,384]{3,2,1,0:T(8,128)(2,1)S(1)}, bf16[1,5,384,384]{3,2,1,0:T(8,128)(2,1)}, u32[]{:S(2)}) %copy-start.4) | copy-done | bytes 1474584
  3.8 0.0 copy-start.1
  3.8 1.1 %shard_map.47 = (bf16[2,384,384]{2,1,0:T(8,128)(2,1)}, bf16[1,384,384]{2,1,0:T(8,128)(2,1)}, bf16[384,384]{1,0:T(8,128)(2,1)}) custom-call(bf16[5,384,384]{2,1,0:T(8,128)(2,1)S(1)} %bitcast.10, bf16[5,384,384]{2,1,0:T(8,128)(2,1)S(1)} %copy-done, bf16[2,384,384]{2,1,0:T(8,128)(2,1)S(1)} %bitcast.4), custom_call_target="tpu_custom_call" | custom-call | flops 147456 | bytes 4000000 | tf_op jit(solution)/shard_map/pallas_call | solution.py:174
  5.0 0.0 copy-start.3
  5.0 0.0 copy-start.5
  5.0 3.7 %collective-permute-start.2 = (bf16[2,384,384]{2,1,0:T(8,128)(2,1)}, bf16[2,384,384]{2,1,0:T(8,128)(2,1)S(1)}, u32[]{:S(2)}, u32[]{:S(2)}) collective-permute-start(bf16[2,384,384]{2,1,0:T(8,128)(2,1)} %get-tuple-element.22), channel_id=1, source_target_pairs={{0,16},{1,17},{2,18},{3,19},{4,20},{5,21},{6,22},{7,23},{8,24},{9,... | collective-permute-start | bytes 1769480 | tf_op jit(solution)/shard_map/ppermute | solution.py:170
  8.6 0.0 copy-done.1
  8.6 1.1 %bitcast_select_fusion = bf16[2,384,384]{2,1,0:T(8,128)(2,1)S(1)} fusion(bf16[1,5,384,384]{3,2,1,0:T(8,128)(2,1)} %param.5, bf16[5,384,384]{2,1,0:T(8,128)(2,1)S(1)} %copy-done.1, pred[]{:T(512)S(6)} %eq.3), kind=kLoop, calls=%fused_computation | loop fusion | flops 294912 | bytes 1769473 | tf_op jit(solution)/shard_map/jit(_where)/select_n | solution.py:173
  9.8 3.5 %collective-permute-start = (bf16[2,384,384]{2,1,0:T(8,128)(2,1)S(1)}, bf16[2,384,384]{2,1,0:T(8,128)(2,1)}, u32[]{:S(2)}, u32[]{:S(2)}) collective-permute-start(bf16[2,384,384]{2,1,0:T(8,128)(2,1)S(1)} %bitcast_select_fusion), channel_id=1, source_target_pairs={{0,16},{1,17},{2,18},{3,19},{4,20},{5,21},{6,22},{7,23},{8,24},{9,... | collective-permute-start | bytes 1769480 | tf_op jit(solution)/shard_map/ppermute | solution.py:170
  13.3 0.0 copy-done.3
  13.4 4.9 %collective-permute-start.4 = (bf16[2,384,384]{2,1,0:T(8,128)(2,1)S(1)}, bf16[2,384,384]{2,1,0:T(8,128)(2,1)S(1)}, u32[]{:S(2)}, u32[]{:S(2)}) collective-permute-start(bf16[2,384,384]{2,1,0:T(8,128)(2,1)S(1)} %bitcast.5), channel_id=1, source_target_pairs={{0,1},{1,2},{2,3},{3,4},{4,5},{5,6},{6,7},{7,8},{8,9},{9,10},{10,1... | collective-permute-start | bytes 1769480 | tf_op jit(solution)/shard_map/ppermute | solution.py:170
  18.2 11.2 %collective-permute-done.2.arr34 = bf16[2,384,384]{2,1,0:T(8,128)(2,1)S(1)} collective-permute-done((bf16[2,384,384]{2,1,0:T(8,128)(2,1)}, bf16[2,384,384]{2,1,0:T(8,128)(2,1)S(1)}, u32[]{:S(2)}, u32[]{:S(2)}) %collective-permute-start.2) | collective-permute-done | bytes 589856 | tf_op jit(solution)/shard_map/ppermute | solution.py:170
  29.4 6.1 %collective-permute-start.3 = (bf16[2,384,384]{2,1,0:T(8,128)(2,1)S(1)}, bf16[2,384,384]{2,1,0:T(8,128)(2,1)}, u32[]{:S(2)}, u32[]{:S(2)}) collective-permute-start(bf16[2,384,384]{2,1,0:T(8,128)(2,1)S(1)} %collective-permute-done.2.arr34), channel_id=1, source_target_pairs={{16,17},{17,18},{18,19},{19,20},{20,21},{21,22},{22,23},{23,24},{2... | collective-permute-start | bytes 1769480 | tf_op jit(solution)/shard_map/ppermute | solution.py:170
  35.5 6.7 %collective-permute-done.arr10 = bf16[2,384,384]{2,1,0:T(8,128)(2,1)} collective-permute-done((bf16[2,384,384]{2,1,0:T(8,128)(2,1)S(1)}, bf16[2,384,384]{2,1,0:T(8,128)(2,1)}, u32[]{:S(2)}, u32[]{:S(2)}) %collective-permute-start) | collective-permute-done | bytes 589856 | tf_op jit(solution)/shard_map/ppermute | solution.py:170
  42.2 5.2 %collective-permute-start.1 = (bf16[2,384,384]{2,1,0:T(8,128)(2,1)}, bf16[2,384,384]{2,1,0:T(8,128)(2,1)}, u32[]{:S(2)}, u32[]{:S(2)}) collective-permute-start(bf16[2,384,384]{2,1,0:T(8,128)(2,1)} %collective-permute-done.arr10), channel_id=1, source_target_pairs={{16,17},{17,18},{18,19},{19,20},{20,21},{21,22},{22,23},{23,24},{2... | collective-permute-start | bytes 1769480 | tf_op jit(solution)/shard_map/ppermute | solution.py:170
  47.4 1.9 %collective-permute-start.5 = (bf16[1,384,384]{2,1,0:T(8,128)(2,1)}, bf16[1,384,384]{2,1,0:T(8,128)(2,1)S(1)}, u32[]{:S(2)}, u32[]{:S(2)}) collective-permute-start(bf16[1,384,384]{2,1,0:T(8,128)(2,1)} %get-tuple-element.27), channel_id=1, source_target_pairs={{0,16},{1,17},{2,18},{3,19},{4,20},{5,21},{6,22},{7,23},{8,24},{9,... | collective-permute-start | bytes 884744 | tf_op jit(solution)/shard_map/ppermute | solution.py:170
  49.4 1.9 %collective-permute-start.6 = (bf16[384,384]{1,0:T(8,128)(2,1)}, bf16[384,384]{1,0:T(8,128)(2,1)}, u32[]{:S(2)}, u32[]{:S(2)}) collective-permute-start(bf16[384,384]{1,0:T(8,128)(2,1)} %get-tuple-element.28), channel_id=1, source_target_pairs={{0,15},{1,0},{2,1},{3,2},{4,3},{5,4},{6,5},{7,6},{8,7},{9,8},{10,9... | collective-permute-start | bytes 884744 | tf_op jit(solution)/shard_map/ppermute | solution.py:170
  51.3 0.0 copy-done.5
  51.3 0.7 %copy.7 = f32[1,5,5,2,2]{4,3,2,1,0:T(2,128)} copy(f32[1,5,5,2,2]{2,4,3,1,0:T(2,128)S(1)} %copy-done.5) | data formatting | bytes 800 | tf_op args[2]
  52.0 0.9 %reshape.4.k = f32[100]{0:T(128)S(1)} reshape(f32[1,5,5,2,2]{4,3,2,1,0:T(2,128)} %copy.7) | data formatting | bytes 800 | tf_op jit(solution)/shard_map/reshape | solution.py:166
  52.9 1.6 %shard_map.46 = (bf16[2,384,384]{2,1,0:T(8,128)(2,1)S(1)}, bf16[2,384,384]{2,1,0:T(8,128)(2,1)S(1)}, f32[3,384,384]{2,1,0:T(8,128)S(1)}, f32[384,384]{1,0:T(8,128)S(1)}, bf16[2,384,384]{2,1,0:T(8,128)(2,1)S(1)}) custom-call(f32[100]{0:T(128)S(1)} %reshape.4.k, bf16[5,384,384]{2,1,0:T(8,128)(2,1)S(1)} %copy-done.1, ...), custom_call_target="tpu_custom_call" | custom-call | flops 113246208 | bytes 4000000 | tf_op jit(solution)/shard_map/pallas_call | solution.py:183
  54.5 0.0 collective-permute-done.4.near
  54.5 1.3 %shard_map.48 = (f32[3,384,384]{2,1,0:T(8,128)S(1)}, f32[384,384]{1,0:T(8,128)S(1)}, bf16[384,384]{1,0:T(8,128)(2,1)S(1)}) custom-call(f32[100]{0:T(128)S(1)} %reshape.4.k, bf16[5,384,384]{2,1,0:T(8,128)(2,1)S(1)} %copy-done.1, bf16[2,384,384]{2,1,0:T(8,128)(2,1)S(1)} %collective-permute-done.2.arr34, bf16[2,384,384]{2,1,0:T(8,128)(2,1)S(1)} %bitcast.7, ...), custom_call_target="tpu_custom_call" | custom-call | flops 226492416 | bytes 4000000 | tf_op jit(solution)/shard_map/pallas_call | solution.py:191
  55.8 3.1 %collective-permute-done.5.arr2 = bf16[1,384,384]{2,1,0:T(8,128)(2,1)S(1)} collective-permute-done((bf16[1,384,384]{2,1,0:T(8,128)(2,1)}, bf16[1,384,384]{2,1,0:T(8,128)(2,1)S(1)}, u32[]{:S(2)}, u32[]{:S(2)}) %collective-permute-start.5) | collective-permute-done | bytes 294944 | tf_op jit(solution)/shard_map/ppermute | solution.py:170
  58.9 1.2 %shard_map.49 = (bf16[384,384]{1,0:T(8,128)(2,1)S(1)}, f32[384,384]{1,0:T(8,128)S(1)}) custom-call(f32[100]{0:T(128)S(1)} %reshape.4.k, bf16[5,384,384]{2,1,0:T(8,128)(2,1)S(1)} %copy-done.1, bf16[1,384,384]{2,1,0:T(8,128)(2,1)S(1)} %collective-permute-done.5.arr2, bf16[2,384,384]{2,1,0:T(8,128)(2,1)S(1)} %collective-permute-done.4.near, ...), custom_call_target="tpu_custom_call" | custom-call | flops 226492416 | bytes 4000000 | tf_op jit(solution)/shard_map/pallas_call | solution.py:198
  60.1 4.5 %collective-permute-start.7 = (bf16[384,384]{1,0:T(8,128)(2,1)S(1)}, bf16[384,384]{1,0:T(8,128)(2,1)S(1)}, u32[]{:S(2)}, u32[]{:S(2)}) collective-permute-start(bf16[384,384]{1,0:T(8,128)(2,1)S(1)} %get-tuple-element.36), channel_id=1, source_target_pairs={{0,1},{1,2},{2,3},{3,4},{4,5},{5,6},{6,7},{7,8},{8,9},{9,10},{10,1... | collective-permute-start | bytes 884744 | tf_op jit(solution)/shard_map/ppermute | solution.py:170
  64.7 0.0 collective-permute-done.6.up
  64.7 2.8 %shard_map.50 = (f32[3,384,384]{2,1,0:T(8,128)S(1)}, f32[384,384]{1,0:T(8,128)S(1)}, f32[384,384]{1,0:T(8,128)S(1)}) custom-call(f32[100]{0:T(128)S(1)} %reshape.4.k, bf16[5,384,384]{2,1,0:T(8,128)(2,1)S(1)} %copy-done.1, bf16[2,384,384]{2,1,0:T(8,128)(2,1)S(1)} %get-tuple-element.26.e01, bf16[2,384,384]{2,1,0:T(8,128)(2,1)S(1)} %collective-permute-done.2.arr34, ...), custom_call_target="tpu_custom_call" | custom-call | flops 905969664 | bytes 4000000 | tf_op jit(solution)/shard_map/pallas_call | solution.py:202
  67.5 0.0 collective-permute-done.3.got34
  67.5 0.0 collective-permute-done.1.got10
  67.5 4.2 %shard_map.51.out_in = bf16[1,5,384,384]{3,2,1,0:T(8,128)(2,1)} custom-call(f32[100]{0:T(128)S(1)} %reshape.4.k, bf16[2,384,384]{2,1,0:T(8,128)(2,1)S(1)} %get-tuple-element.21.h01, bf16[2,384,384]{2,1,0:T(8,128)(2,1)} %collective-permute-done.1.got10, bf16[2,384,384]{2,1,0:T(8,128)(2,1)S(1)} %collective-permute-done.2.arr34, ...), custom_call_target="tpu_custom_call" | custom-call | flops 1019215872 | bytes 4000000 | tf_op jit(solution)/shard_map/pallas_call | solution.py:205
  71.7 0.0 collective-permute-done.7.c2
  71.7 0.8 %finish.1 = bf16[1,5,384,384]{3,2,1,0:T(8,128)(2,1)} custom-call(bf16[1,5,384,384]{3,2,1,0:T(8,128)(2,1)} %shard_map.51.out_in, f32[384,384]{1,0:T(8,128)S(1)} %get-tuple-element.35.p0, bf16[384,384]{1,0:T(8,128)(2,1)S(1)} %collective-permute-done.7.c2), custom_call_target="tpu_custom_call", output_to_operand_aliasing={{}: (0, {})} | custom-call | flops 147456 | bytes 1000000 | tf_op jit(solution)/shard_map/finish/pallas_call | solution.py:217
Async XLA Ops:
  0.0 1.4 %copy-start = (bf16[5,384,384]{2,1,0:T(8,128)(2,1)S(1)}, bf16[5,384,384]{2,1,0:T(8,128)(2,1)}, u32[]{:S(2)}) copy-start(bf16[5,384,384]{2,1,0:T(8,128)(2,1)} %bnd.9) | copy-start | bytes 4423684
  1.4 1.1 %copy-start.2 = (bf16[1,2,384,384]{3,2,1,0:T(8,128)(2,1)S(1)}, bf16[1,2,384,384]{3,2,1,0:T(8,128)(2,1)}, u32[]{:S(2)}) copy-start(bf16[1,2,384,384]{3,2,1,0:T(8,128)(2,1)} %param.4) | copy-start | bytes 1769476
  2.4 1.4 %copy-start.4 = (bf16[1,5,384,384]{3,2,1,0:T(8,128)(2,1)S(1)}, bf16[1,5,384,384]{3,2,1,0:T(8,128)(2,1)}, u32[]{:S(2)}) copy-start(bf16[1,5,384,384]{3,2,1,0:T(8,128)(2,1)} %param.5) | copy-start | bytes 4423684
  3.8 4.8 %copy-start.1 = (bf16[5,384,384]{2,1,0:T(8,128)(2,1)S(1)}, bf16[5,384,384]{2,1,0:T(8,128)(2,1)}, u32[]{:S(2)}) copy-start(bf16[5,384,384]{2,1,0:T(8,128)(2,1)} %bnd.9) | copy-start | bytes 4423684
  5.0 8.4 %copy-start.3 = (bf16[1,2,384,384]{3,2,1,0:T(8,128)(2,1)S(1)}, bf16[1,2,384,384]{3,2,1,0:T(8,128)(2,1)}, u32[]{:S(2)}) copy-start(bf16[1,2,384,384]{3,2,1,0:T(8,128)(2,1)} %param.4) | copy-start | bytes 1769476
  5.0 46.3 %copy-start.5 = (f32[1,5,5,2,2]{2,4,3,1,0:T(2,128)S(1)}, f32[1,5,5,2,2]{2,4,3,1,0:T(2,128)}, u32[]{:S(2)}) copy-start(f32[1,5,5,2,2]{2,4,3,1,0:T(2,128)} %param.6) | copy-start | bytes 1204
  5.0 24.5 %collective-permute-start.2 = (bf16[2,384,384]{2,1,0:T(8,128)(2,1)}, bf16[2,384,384]{2,1,0:T(8,128)(2,1)S(1)}, u32[]{:S(2)}, u32[]{:S(2)}) collective-permute-start(bf16[2,384,384]{2,1,0:T(8,128)(2,1)} %get-tuple-element.22), channel_id=1, source_target_pairs={{0,16},{1,17},{2,18},{3,19},{4,20},{5,21},{6,22},{7,23},{8,24},{9,... | collective-permute-start | bytes 1769480 | tf_op jit(solution)/shard_map/ppermute | solution.py:170
  9.8 32.4 %collective-permute-start = (bf16[2,384,384]{2,1,0:T(8,128)(2,1)S(1)}, bf16[2,384,384]{2,1,0:T(8,128)(2,1)}, u32[]{:S(2)}, u32[]{:S(2)}) collective-permute-start(bf16[2,384,384]{2,1,0:T(8,128)(2,1)S(1)} %bitcast_select_fusion), channel_id=1, source_target_pairs={{0,16},{1,17},{2,18},{3,19},{4,20},{5,21},{6,22},{7,23},{8,24},{9,... | collective-permute-start | bytes 1769480 | tf_op jit(solution)/shard_map/ppermute | solution.py:170
  13.4 41.1 %collective-permute-start.4 = (bf16[2,384,384]{2,1,0:T(8,128)(2,1)S(1)}, bf16[2,384,384]{2,1,0:T(8,128)(2,1)S(1)}, u32[]{:S(2)}, u32[]{:S(2)}) collective-permute-start(bf16[2,384,384]{2,1,0:T(8,128)(2,1)S(1)} %bitcast.5), channel_id=1, source_target_pairs={{0,1},{1,2},{2,3},{3,4},{4,5},{5,6},{6,7},{7,8},{8,9},{9,10},{10,1... | collective-permute-start | bytes 1769480 | tf_op jit(solution)/shard_map/ppermute | solution.py:170
  29.4 38.0 %collective-permute-start.3 = (bf16[2,384,384]{2,1,0:T(8,128)(2,1)S(1)}, bf16[2,384,384]{2,1,0:T(8,128)(2,1)}, u32[]{:S(2)}, u32[]{:S(2)}) collective-permute-start(bf16[2,384,384]{2,1,0:T(8,128)(2,1)S(1)} %collective-permute-done.2.arr34), channel_id=1, source_target_pairs={{16,17},{17,18},{18,19},{19,20},{20,21},{21,22},{22,23},{23,24},{2... | collective-permute-start | bytes 1769480 | tf_op jit(solution)/shard_map/ppermute | solution.py:170
  42.2 25.3 %collective-permute-start.1 = (bf16[2,384,384]{2,1,0:T(8,128)(2,1)}, bf16[2,384,384]{2,1,0:T(8,128)(2,1)}, u32[]{:S(2)}, u32[]{:S(2)}) collective-permute-start(bf16[2,384,384]{2,1,0:T(8,128)(2,1)} %collective-permute-done.arr10), channel_id=1, source_target_pairs={{16,17},{17,18},{18,19},{19,20},{20,21},{21,22},{22,23},{23,24},{2... | collective-permute-start | bytes 1769480 | tf_op jit(solution)/shard_map/ppermute | solution.py:170
  47.4 11.5 %collective-permute-start.5 = (bf16[1,384,384]{2,1,0:T(8,128)(2,1)}, bf16[1,384,384]{2,1,0:T(8,128)(2,1)S(1)}, u32[]{:S(2)}, u32[]{:S(2)}) collective-permute-start(bf16[1,384,384]{2,1,0:T(8,128)(2,1)} %get-tuple-element.27), channel_id=1, source_target_pairs={{0,16},{1,17},{2,18},{3,19},{4,20},{5,21},{6,22},{7,23},{8,24},{9,... | collective-permute-start | bytes 884744 | tf_op jit(solution)/shard_map/ppermute | solution.py:170
  49.4 15.3 %collective-permute-start.6 = (bf16[384,384]{1,0:T(8,128)(2,1)}, bf16[384,384]{1,0:T(8,128)(2,1)}, u32[]{:S(2)}, u32[]{:S(2)}) collective-permute-start(bf16[384,384]{1,0:T(8,128)(2,1)} %get-tuple-element.28), channel_id=1, source_target_pairs={{0,15},{1,0},{2,1},{3,2},{4,3},{5,4},{6,5},{7,6},{8,7},{9,8},{10,9... | collective-permute-start | bytes 884744 | tf_op jit(solution)/shard_map/ppermute | solution.py:170
  60.1 11.6 %collective-permute-start.7 = (bf16[384,384]{1,0:T(8,128)(2,1)S(1)}, bf16[384,384]{1,0:T(8,128)(2,1)S(1)}, u32[]{:S(2)}, u32[]{:S(2)}) collective-permute-start(bf16[384,384]{1,0:T(8,128)(2,1)S(1)} %get-tuple-element.36), channel_id=1, source_target_pairs={{0,1},{1,2},{2,3},{3,4},{4,5},{5,6},{6,7},{7,8},{8,9},{9,10},{10,1... | collective-permute-start | bytes 884744 | tf_op jit(solution)/shard_map/ppermute | solution.py:170

commit v4 on v3

--- a/solution.py
+++ b/solution.py
@@ -89,7 +89,7 @@
     c2[...] = dot(own_t[1], z).astype(BF16)
 
 
-def late(k, bnd, e01, arr34, arr2, own, near, up, own_t, z034_in, y2, p0, last, p1):
+def late(k, bnd, e01, arr34, arr2, own, near, own_t, z034_in, y2, p0, last, z1):
     first = lax.axis_index("site") == 0
     e0 = e01[0].astype(F32)
     e3 = jnp.where(first, bnd[3], arr34[0]).astype(F32)
@@ -102,11 +102,10 @@
     for i, v in enumerate(FLAT):
         z = (z034_in[i] + coupling(k, 2, v, 0, 1) * y2[...]).astype(BF16)
         p0[i] = dot(own_t[0], z)
-    y = coupling(k, 1, 1, 0, 0) * dot(e01[1], up[...])
-    p1[...] = dot(own_t[0], (dot(e034, own[1]) + y).astype(BF16))
-
-
-def join(k, h01, got10, arr34, got34, own, near, near_t, p0, p1, out, y, done, sems):
+    z1[...] = dot(e034, own[1])
+
+
+def join(k, h01, got10, arr34, got34, e01, up, own, own_t, near, near_t, p0, z1, out, y, done, sems):
     copies = []
 
     def store(v, total):
@@ -120,7 +119,8 @@
     y[0] = dot(jnp.where(first, h01[0], got10[0]), near[1])
     y[1] = dot(f1, own[0])
     carried = dot(near_t[...], (coupling(k, 1, 1, 1, 1) * dot(f1, own[1])).astype(BF16))
-    store(1, p1[...] + carried.astype(BF16).astype(F32))
+    z = z1[...] + coupling(k, 1, 1, 0, 0) * dot(e01[1], up[...])
+    store(1, dot(own_t[0], z.astype(BF16)) + carried.astype(BF16).astype(F32))
     y[2] = dot(jnp.where(first, arr34[0], got34[0]), near[1])
     y[3] = dot(jnp.where(first, arr34[1], got34[1]), near[1])
     for i, v in enumerate(FLAT):
@@ -199,21 +199,21 @@
         send, [(block, BF16), (block, F32)], 2 * flop, [scalars()] + [v] * 5
     )(k, boundary, arr2, near, own_t, c2)
     c2 = send_on(c2, ahead)
-    p0, tail, p1 = kernel_call(
-        late, [((3, *block), F32), (block, F32), (block, F32)], 8 * flop, [scalars()] + [v] * 10
-    )(k, boundary, e01, arr34, arr2, own, near, up, own_t, z034, y2)
+    p0, tail, z1 = kernel_call(
+        late, [((3, *block), F32), (block, F32), (block, F32)], 6 * flop, [scalars()] + [v] * 9
+    )(k, boundary, e01, arr34, arr2, own, near, own_t, z034, y2)
     (out,) = kernel_call(
         join,
         [((1, 5, *block), BF16)],
-        9 * flop,
-        [scalars()] + [v] * 9,
+        11 * flop,
+        [scalars()] + [v] * 12,
         [
             pltpu.VMEM((4, *block), F32),
             pltpu.VMEM((4, *block), BF16),
             pltpu.SemaphoreType.DMA((4,)),
         ],
         place=pltpu.HBM,
-    )(k, h01, got10, arr34, got34, own, near, near_t, p0, p1)
+    )(k, h01, got10, arr34, got34, e01, up, own, own_t, near, near_t, p0, z1)
     (out,) = pl.pallas_call(
         finish,
         out_shape=[jax.ShapeDtypeStruct((1, 5, *block), BF16)],

time: 73.1 us -> 72.8 us (level)
  no operation moved by 1% of the time
where the time goes in v4:
time: 72.8 us; the launch traced here: 72.2 us
  starting transfers between devices  31.8 us (44%)
  waiting for transfers between devices  21 us (29%)
  Pallas kernels  12.7 us (17%)
  local copies, waits for them, and re-layouts  5.43 us (7%)
  other arithmetic  1.14 us (2%)
    ppermute x8, starting transfers between devices, send_on(): return lax.ppermute(value, AXES, route)  31.8 us
    ppermute x8, waiting for transfers between devices, send_on(): return lax.ppermute(value, AXES, route)  21 us
    pallas_call x1, Pallas kernels, local(): kernel_call(join, [((1, 5, *block), BF16)], 11 * flop, [scalars()] + [v]...  4.76 us
    unnamed x13, local copies, waits for them, and re-layouts  4.57 us
    pallas_call x1, Pallas kernels, local(): kernel_call(late, [((3, *block), F32), (block, F32), (block, F32)], 6 * f...  1.93 us
    pallas_call x1, Pallas kernels, local(): kernel_call(early, [((2, *block), BF16), ((2, *block), BF16), ((3, *block...  1.57 us
  transfers between devices with their start and end apart: 8, of which 3 were waited for; matrix products, arithmetic and copies ran while one was open for 4% of the time, Pallas kernels for 15%

profile of v4, /device:TPU:27, one launch (start us, length us, event | category | flops | bytes accessed | tf_op | source)
XLA Modules:
  0.0 72.2 jit_solution(521332439652045828)
XLA Ops:
  0.0 0.0 copy-start
  0.0 1.4 %copy-done = bf16[5,384,384]{2,1,0:T(8,128)(2,1)S(1)} copy-done((bf16[5,384,384]{2,1,0:T(8,128)(2,1)S(1)}, bf16[5,384,384]{2,1,0:T(8,128)(2,1)}, u32[]{:S(2)}) %copy-start) | copy-done | bytes 1474584
  1.4 0.0 copy-start.2
  1.4 1.1 %copy-done.2 = bf16[1,2,384,384]{3,2,1,0:T(8,128)(2,1)S(1)} copy-done((bf16[1,2,384,384]{3,2,1,0:T(8,128)(2,1)S(1)}, bf16[1,2,384,384]{3,2,1,0:T(8,128)(2,1)}, u32[]{:S(2)}) %copy-start.2) | copy-done | bytes 589848
  2.4 0.0 copy-start.4
  2.4 1.4 %copy-done.4 = bf16[1,5,384,384]{3,2,1,0:T(8,128)(2,1)S(1)} copy-done((bf16[1,5,384,384]{3,2,1,0:T(8,128)(2,1)S(1)}, bf16[1,5,384,384]{3,2,1,0:T(8,128)(2,1)}, u32[]{:S(2)}) %copy-start.4) | copy-done | bytes 1474584
  3.8 0.0 copy-start.1
  3.8 1.1 %shard_map.47 = (bf16[2,384,384]{2,1,0:T(8,128)(2,1)}, bf16[1,384,384]{2,1,0:T(8,128)(2,1)}, bf16[384,384]{1,0:T(8,128)(2,1)}) custom-call(bf16[5,384,384]{2,1,0:T(8,128)(2,1)S(1)} %bitcast.10, bf16[5,384,384]{2,1,0:T(8,128)(2,1)S(1)} %copy-done, bf16[2,384,384]{2,1,0:T(8,128)(2,1)S(1)} %bitcast.4), custom_call_target="tpu_custom_call" | custom-call | flops 147456 | bytes 4000000 | tf_op jit(solution)/shard_map/pallas_call | solution.py:174
  5.0 0.0 copy-start.3
  5.0 0.0 copy-start.5
  5.0 3.7 %collective-permute-start.2 = (bf16[2,384,384]{2,1,0:T(8,128)(2,1)}, bf16[2,384,384]{2,1,0:T(8,128)(2,1)S(1)}, u32[]{:S(2)}, u32[]{:S(2)}) collective-permute-start(bf16[2,384,384]{2,1,0:T(8,128)(2,1)} %get-tuple-element.22), channel_id=1, source_target_pairs={{0,16},{1,17},{2,18},{3,19},{4,20},{5,21},{6,22},{7,23},{8,24},{9,... | collective-permute-start | bytes 1769480 | tf_op jit(solution)/shard_map/ppermute | solution.py:170
  8.6 0.0 copy-done.1
  8.6 1.1 %bitcast_select_fusion = bf16[2,384,384]{2,1,0:T(8,128)(2,1)S(1)} fusion(bf16[1,5,384,384]{3,2,1,0:T(8,128)(2,1)} %param.5, bf16[5,384,384]{2,1,0:T(8,128)(2,1)S(1)} %copy-done.1, pred[]{:T(512)S(6)} %eq.3), kind=kLoop, calls=%fused_computation | loop fusion | flops 294912 | bytes 1769473 | tf_op jit(solution)/shard_map/jit(_where)/select_n | solution.py:173
  9.8 3.5 %collective-permute-start = (bf16[2,384,384]{2,1,0:T(8,128)(2,1)S(1)}, bf16[2,384,384]{2,1,0:T(8,128)(2,1)}, u32[]{:S(2)}, u32[]{:S(2)}) collective-permute-start(bf16[2,384,384]{2,1,0:T(8,128)(2,1)S(1)} %bitcast_select_fusion), channel_id=1, source_target_pairs={{0,16},{1,17},{2,18},{3,19},{4,20},{5,21},{6,22},{7,23},{8,24},{9,... | collective-permute-start | bytes 1769480 | tf_op jit(solution)/shard_map/ppermute | solution.py:170
  13.3 0.0 copy-done.3
  13.4 4.9 %collective-permute-start.5 = (bf16[2,384,384]{2,1,0:T(8,128)(2,1)S(1)}, bf16[2,384,384]{2,1,0:T(8,128)(2,1)S(1)}, u32[]{:S(2)}, u32[]{:S(2)}) collective-permute-start(bf16[2,384,384]{2,1,0:T(8,128)(2,1)S(1)} %bitcast.5), channel_id=1, source_target_pairs={{0,1},{1,2},{2,3},{3,4},{4,5},{5,6},{6,7},{7,8},{8,9},{9,10},{10,1... | collective-permute-start | bytes 1769480 | tf_op jit(solution)/shard_map/ppermute | solution.py:170
  18.2 11.2 %collective-permute-done.2.arr34 = bf16[2,384,384]{2,1,0:T(8,128)(2,1)S(1)} collective-permute-done((bf16[2,384,384]{2,1,0:T(8,128)(2,1)}, bf16[2,384,384]{2,1,0:T(8,128)(2,1)S(1)}, u32[]{:S(2)}, u32[]{:S(2)}) %collective-permute-start.2) | collective-permute-done | bytes 589856 | tf_op jit(solution)/shard_map/ppermute | solution.py:170
  29.4 6.1 %collective-permute-start.3 = (bf16[2,384,384]{2,1,0:T(8,128)(2,1)S(1)}, bf16[2,384,384]{2,1,0:T(8,128)(2,1)}, u32[]{:S(2)}, u32[]{:S(2)}) collective-permute-start(bf16[2,384,384]{2,1,0:T(8,128)(2,1)S(1)} %collective-permute-done.2.arr34), channel_id=1, source_target_pairs={{16,17},{17,18},{18,19},{19,20},{20,21},{21,22},{22,23},{23,24},{2... | collective-permute-start | bytes 1769480 | tf_op jit(solution)/shard_map/ppermute | solution.py:170
  35.5 6.7 %collective-permute-done.arr10 = bf16[2,384,384]{2,1,0:T(8,128)(2,1)} collective-permute-done((bf16[2,384,384]{2,1,0:T(8,128)(2,1)S(1)}, bf16[2,384,384]{2,1,0:T(8,128)(2,1)}, u32[]{:S(2)}, u32[]{:S(2)}) %collective-permute-start) | collective-permute-done | bytes 589856 | tf_op jit(solution)/shard_map/ppermute | solution.py:170
  42.2 5.2 %collective-permute-start.1 = (bf16[2,384,384]{2,1,0:T(8,128)(2,1)}, bf16[2,384,384]{2,1,0:T(8,128)(2,1)}, u32[]{:S(2)}, u32[]{:S(2)}) collective-permute-start(bf16[2,384,384]{2,1,0:T(8,128)(2,1)} %collective-permute-done.arr10), channel_id=1, source_target_pairs={{16,17},{17,18},{18,19},{19,20},{20,21},{21,22},{22,23},{23,24},{2... | collective-permute-start | bytes 1769480 | tf_op jit(solution)/shard_map/ppermute | solution.py:170
  47.4 1.9 %collective-permute-start.6 = (bf16[1,384,384]{2,1,0:T(8,128)(2,1)}, bf16[1,384,384]{2,1,0:T(8,128)(2,1)S(1)}, u32[]{:S(2)}, u32[]{:S(2)}) collective-permute-start(bf16[1,384,384]{2,1,0:T(8,128)(2,1)} %get-tuple-element.29), channel_id=1, source_target_pairs={{0,16},{1,17},{2,18},{3,19},{4,20},{5,21},{6,22},{7,23},{8,24},{9,... | collective-permute-start | bytes 884744 | tf_op jit(solution)/shard_map/ppermute | solution.py:170
  49.4 1.9 %collective-permute-start.4 = (bf16[384,384]{1,0:T(8,128)(2,1)}, bf16[384,384]{1,0:T(8,128)(2,1)}, u32[]{:S(2)}, u32[]{:S(2)}) collective-permute-start(bf16[384,384]{1,0:T(8,128)(2,1)} %get-tuple-element.24), channel_id=1, source_target_pairs={{0,15},{1,0},{2,1},{3,2},{4,3},{5,4},{6,5},{7,6},{8,7},{9,8},{10,9... | collective-permute-start | bytes 884744 | tf_op jit(solution)/shard_map/ppermute | solution.py:170
  51.3 0.0 copy-done.5
  51.3 0.7 %copy.7 = f32[1,5,5,2,2]{4,3,2,1,0:T(2,128)} copy(f32[1,5,5,2,2]{2,4,3,1,0:T(2,128)S(1)} %copy-done.5) | data formatting | bytes 800 | tf_op args[2]
  52.0 0.9 %reshape.4.k = f32[100]{0:T(128)S(1)} reshape(f32[1,5,5,2,2]{4,3,2,1,0:T(2,128)} %copy.7) | data formatting | bytes 800 | tf_op jit(solution)/shard_map/reshape | solution.py:166
  52.9 1.6 %shard_map.46 = (bf16[2,384,384]{2,1,0:T(8,128)(2,1)S(1)}, bf16[2,384,384]{2,1,0:T(8,128)(2,1)S(1)}, f32[3,384,384]{2,1,0:T(8,128)S(1)}, f32[384,384]{1,0:T(8,128)S(1)}, bf16[2,384,384]{2,1,0:T(8,128)(2,1)S(1)}) custom-call(f32[100]{0:T(128)S(1)} %reshape.4.k, bf16[5,384,384]{2,1,0:T(8,128)(2,1)S(1)} %copy-done.1, ...), custom_call_target="tpu_custom_call" | custom-call | flops 113246208 | bytes 4000000 | tf_op jit(solution)/shard_map/pallas_call | solution.py:183
  54.5 0.0 collective-permute-done.5.near
  54.5 1.3 %shard_map.48 = (f32[3,384,384]{2,1,0:T(8,128)S(1)}, f32[384,384]{1,0:T(8,128)S(1)}, bf16[384,384]{1,0:T(8,128)(2,1)S(1)}) custom-call(f32[100]{0:T(128)S(1)} %reshape.4.k, bf16[5,384,384]{2,1,0:T(8,128)(2,1)S(1)} %copy-done.1, bf16[2,384,384]{2,1,0:T(8,128)(2,1)S(1)} %collective-permute-done.2.arr34, bf16[2,384,384]{2,1,0:T(8,128)(2,1)S(1)} %bitcast.7, ...), custom_call_target="tpu_custom_call" | custom-call | flops 226492416 | bytes 4000000 | tf_op jit(solution)/shard_map/pallas_call | solution.py:191
  55.8 3.1 %collective-permute-done.6.arr2 = bf16[1,384,384]{2,1,0:T(8,128)(2,1)S(1)} collective-permute-done((bf16[1,384,384]{2,1,0:T(8,128)(2,1)}, bf16[1,384,384]{2,1,0:T(8,128)(2,1)S(1)}, u32[]{:S(2)}, u32[]{:S(2)}) %collective-permute-start.6) | collective-permute-done | bytes 294944 | tf_op jit(solution)/shard_map/ppermute | solution.py:170
  58.9 1.2 %shard_map.49 = (bf16[384,384]{1,0:T(8,128)(2,1)S(1)}, f32[384,384]{1,0:T(8,128)S(1)}) custom-call(f32[100]{0:T(128)S(1)} %reshape.4.k, bf16[5,384,384]{2,1,0:T(8,128)(2,1)S(1)} %copy-done.1, bf16[1,384,384]{2,1,0:T(8,128)(2,1)S(1)} %collective-permute-done.6.arr2, bf16[2,384,384]{2,1,0:T(8,128)(2,1)S(1)} %collective-permute-done.5.near, ...), custom_call_target="tpu_custom_call" | custom-call | flops 226492416 | bytes 4000000 | tf_op jit(solution)/shard_map/pallas_call | solution.py:198
  60.1 4.5 %collective-permute-start.7 = (bf16[384,384]{1,0:T(8,128)(2,1)S(1)}, bf16[384,384]{1,0:T(8,128)(2,1)S(1)}, u32[]{:S(2)}, u32[]{:S(2)}) collective-permute-start(bf16[384,384]{1,0:T(8,128)(2,1)S(1)} %get-tuple-element.36), channel_id=1, source_target_pairs={{0,1},{1,2},{2,3},{3,4},{4,5},{5,6},{6,7},{7,8},{8,9},{9,10},{10,1... | collective-permute-start | bytes 884744 | tf_op jit(solution)/shard_map/ppermute | solution.py:170
  64.7 1.9 %shard_map.50 = (f32[3,384,384]{2,1,0:T(8,128)S(1)}, f32[384,384]{1,0:T(8,128)S(1)}, f32[384,384]{1,0:T(8,128)S(1)}) custom-call(f32[100]{0:T(128)S(1)} %reshape.4.k, bf16[5,384,384]{2,1,0:T(8,128)(2,1)S(1)} %copy-done.1, bf16[2,384,384]{2,1,0:T(8,128)(2,1)S(1)} %get-tuple-element.23.e01, bf16[2,384,384]{2,1,0:T(8,128)(2,1)S(1)} %collective-permute-done.2.arr34, ...), custom_call_target="tpu_custom_call" | custom-call | flops 679477248 | bytes 4000000 | tf_op jit(solution)/shard_map/pallas_call | solution.py:202
  66.6 0.0 collective-permute-done.4.up
  66.6 0.0 collective-permute-done.3.got34
  66.6 0.0 collective-permute-done.1.got10
  66.6 4.8 %shard_map.51.out_in = bf16[1,5,384,384]{3,2,1,0:T(8,128)(2,1)} custom-call(f32[100]{0:T(128)S(1)} %reshape.4.k, bf16[2,384,384]{2,1,0:T(8,128)(2,1)S(1)} %get-tuple-element.21.h01, bf16[2,384,384]{2,1,0:T(8,128)(2,1)} %collective-permute-done.1.got10, bf16[2,384,384]{2,1,0:T(8,128)(2,1)S(1)} %collective-permute-done.2.arr34, ...), custom_call_target="tpu_custom_call" | custom-call | flops 1245708288 | bytes 4000000 | tf_op jit(solution)/shard_map/pallas_call | solution.py:205
  71.4 0.0 collective-permute-done.7.c2
  71.4 0.8 %finish.1 = bf16[1,5,384,384]{3,2,1,0:T(8,128)(2,1)} custom-call(bf16[1,5,384,384]{3,2,1,0:T(8,128)(2,1)} %shard_map.51.out_in, f32[384,384]{1,0:T(8,128)S(1)} %get-tuple-element.35.p0, bf16[384,384]{1,0:T(8,128)(2,1)S(1)} %collective-permute-done.7.c2), custom_call_target="tpu_custom_call", output_to_operand_aliasing={{}: (0, {})} | custom-call | flops 147456 | bytes 1000000 | tf_op jit(solution)/shard_map/finish/pallas_call | solution.py:217
Async XLA Ops:
  0.0 1.4 %copy-start = (bf16[5,384,384]{2,1,0:T(8,128)(2,1)S(1)}, bf16[5,384,384]{2,1,0:T(8,128)(2,1)}, u32[]{:S(2)}) copy-start(bf16[5,384,384]{2,1,0:T(8,128)(2,1)} %bnd.9) | copy-start | bytes 4423684
  1.4 1.1 %copy-start.2 = (bf16[1,2,384,384]{3,2,1,0:T(8,128)(2,1)S(1)}, bf16[1,2,384,384]{3,2,1,0:T(8,128)(2,1)}, u32[]{:S(2)}) copy-start(bf16[1,2,384,384]{3,2,1,0:T(8,128)(2,1)} %param.4) | copy-start | bytes 1769476
  2.4 1.4 %copy-start.4 = (bf16[1,5,384,384]{3,2,1,0:T(8,128)(2,1)S(1)}, bf16[1,5,384,384]{3,2,1,0:T(8,128)(2,1)}, u32[]{:S(2)}) copy-start(bf16[1,5,384,384]{3,2,1,0:T(8,128)(2,1)} %param.5) | copy-start | bytes 4423684
  3.8 4.8 %copy-start.1 = (bf16[5,384,384]{2,1,0:T(8,128)(2,1)S(1)}, bf16[5,384,384]{2,1,0:T(8,128)(2,1)}, u32[]{:S(2)}) copy-start(bf16[5,384,384]{2,1,0:T(8,128)(2,1)} %bnd.9) | copy-start | bytes 4423684
  5.0 8.4 %copy-start.3 = (bf16[1,2,384,384]{3,2,1,0:T(8,128)(2,1)S(1)}, bf16[1,2,384,384]{3,2,1,0:T(8,128)(2,1)}, u32[]{:S(2)}) copy-start(bf16[1,2,384,384]{3,2,1,0:T(8,128)(2,1)} %param.4) | copy-start | bytes 1769476
  5.0 46.3 %copy-start.5 = (f32[1,5,5,2,2]{2,4,3,1,0:T(2,128)S(1)}, f32[1,5,5,2,2]{2,4,3,1,0:T(2,128)}, u32[]{:S(2)}) copy-start(f32[1,5,5,2,2]{2,4,3,1,0:T(2,128)} %param.6) | copy-start | bytes 1204
  5.0 24.5 %collective-permute-start.2 = (bf16[2,384,384]{2,1,0:T(8,128)(2,1)}, bf16[2,384,384]{2,1,0:T(8,128)(2,1)S(1)}, u32[]{:S(2)}, u32[]{:S(2)}) collective-permute-start(bf16[2,384,384]{2,1,0:T(8,128)(2,1)} %get-tuple-element.22), channel_id=1, source_target_pairs={{0,16},{1,17},{2,18},{3,19},{4,20},{5,21},{6,22},{7,23},{8,24},{9,... | collective-permute-start | bytes 1769480 | tf_op jit(solution)/shard_map/ppermute | solution.py:170
  9.8 32.4 %collective-permute-start = (bf16[2,384,384]{2,1,0:T(8,128)(2,1)S(1)}, bf16[2,384,384]{2,1,0:T(8,128)(2,1)}, u32[]{:S(2)}, u32[]{:S(2)}) collective-permute-start(bf16[2,384,384]{2,1,0:T(8,128)(2,1)S(1)} %bitcast_select_fusion), channel_id=1, source_target_pairs={{0,16},{1,17},{2,18},{3,19},{4,20},{5,21},{6,22},{7,23},{8,24},{9,... | collective-permute-start | bytes 1769480 | tf_op jit(solution)/shard_map/ppermute | solution.py:170
  13.4 41.1 %collective-permute-start.5 = (bf16[2,384,384]{2,1,0:T(8,128)(2,1)S(1)}, bf16[2,384,384]{2,1,0:T(8,128)(2,1)S(1)}, u32[]{:S(2)}, u32[]{:S(2)}) collective-permute-start(bf16[2,384,384]{2,1,0:T(8,128)(2,1)S(1)} %bitcast.5), channel_id=1, source_target_pairs={{0,1},{1,2},{2,3},{3,4},{4,5},{5,6},{6,7},{7,8},{8,9},{9,10},{10,1... | collective-permute-start | bytes 1769480 | tf_op jit(solution)/shard_map/ppermute | solution.py:170
  29.4 37.2 %collective-permute-start.3 = (bf16[2,384,384]{2,1,0:T(8,128)(2,1)S(1)}, bf16[2,384,384]{2,1,0:T(8,128)(2,1)}, u32[]{:S(2)}, u32[]{:S(2)}) collective-permute-start(bf16[2,384,384]{2,1,0:T(8,128)(2,1)S(1)} %collective-permute-done.2.arr34), channel_id=1, source_target_pairs={{16,17},{17,18},{18,19},{19,20},{20,21},{21,22},{22,23},{23,24},{2... | collective-permute-start | bytes 1769480 | tf_op jit(solution)/shard_map/ppermute | solution.py:170
  42.2 24.4 %collective-permute-start.1 = (bf16[2,384,384]{2,1,0:T(8,128)(2,1)}, bf16[2,384,384]{2,1,0:T(8,128)(2,1)}, u32[]{:S(2)}, u32[]{:S(2)}) collective-permute-start(bf16[2,384,384]{2,1,0:T(8,128)(2,1)} %collective-permute-done.arr10), channel_id=1, source_target_pairs={{16,17},{17,18},{18,19},{19,20},{20,21},{21,22},{22,23},{23,24},{2... | collective-permute-start | bytes 1769480 | tf_op jit(solution)/shard_map/ppermute | solution.py:170
  47.4 11.5 %collective-permute-start.6 = (bf16[1,384,384]{2,1,0:T(8,128)(2,1)}, bf16[1,384,384]{2,1,0:T(8,128)(2,1)S(1)}, u32[]{:S(2)}, u32[]{:S(2)}) collective-permute-start(bf16[1,384,384]{2,1,0:T(8,128)(2,1)} %get-tuple-element.29), channel_id=1, source_target_pairs={{0,16},{1,17},{2,18},{3,19},{4,20},{5,21},{6,22},{7,23},{8,24},{9,... | collective-permute-start | bytes 884744 | tf_op jit(solution)/shard_map/ppermute | solution.py:170
  49.4 17.2 %collective-permute-start.4 = (bf16[384,384]{1,0:T(8,128)(2,1)}, bf16[384,384]{1,0:T(8,128)(2,1)}, u32[]{:S(2)}, u32[]{:S(2)}) collective-permute-start(bf16[384,384]{1,0:T(8,128)(2,1)} %get-tuple-element.24), channel_id=1, source_target_pairs={{0,15},{1,0},{2,1},{3,2},{4,3},{5,4},{6,5},{7,6},{8,7},{9,8},{10,9... | collective-permute-start | bytes 884744 | tf_op jit(solution)/shard_map/ppermute | solution.py:170
  60.1 11.3 %collective-permute-start.7 = (bf16[384,384]{1,0:T(8,128)(2,1)S(1)}, bf16[384,384]{1,0:T(8,128)(2,1)S(1)}, u32[]{:S(2)}, u32[]{:S(2)}) collective-permute-start(bf16[384,384]{1,0:T(8,128)(2,1)S(1)} %get-tuple-element.36), channel_id=1, source_target_pairs={{0,1},{1,2},{2,3},{3,4},{4,5},{5,6},{6,7},{7,8},{8,9},{9,10},{10,1... | collective-permute-start | bytes 884744 | tf_op jit(solution)/shard_map/ppermute | solution.py:170
